TPU v7x, 128 devices: a whole 4x4x4 slice. The times are simulated.
128 devices in a mesh: lat: 4 (over z), lon: 32 (over x, y, core).
Axes of the slice: x: 4, y: 4, z: 4, core: 2. Of those that a mesh axis runs over, the one named last changes fastest.
Arguments:
- atm_flux: bfloat16 [8, 256, 4096], P(None, 'lat', 'lon'), may hold values from -6 to 6
- sea_mask: int32 [256, 4096], P('lat', 'lon'), may hold values 0 or 1
- src_block: int32 [32768], P(('lat', 'lon')), may hold values from 0 to 63
- dest_dev: int32 [32768, 1], P(('lat', 'lon')), may hold values from 0 to 127; in each aligned block of 256 rows (0 to 255, 256 to 511, ...) at most 4 rows name the same one
- dest_block: int32 [32768], P(('lat', 'lon')), may hold values from 0 to 31
- intersection_weights: bfloat16 [32768, 128, 128], P(('lat', 'lon')), may hold values from -0.5 to 0.5
- coupling: float32 [4, 8], replicated, may hold values from -2 to 2
- inverses: float32 [4, 128, 32, 80, 80], P(None, 'lat', 'lon'), may hold values from -2 to 2
- ocean_state: float32 [4, 80, 128, 4096], P(None, None, 'lat', 'lon'), may hold values from -6 to 6
- depth_levels: int32 [128, 4096], P('lat', 'lon'), may hold values from 0 to 80
Outputs:
- ocean_out: float32 [4, 80, 128, 4096], P(None, None, 'lat', 'lon')
Inputs may be any that keep to these rules, and one draw needn't show every extreme that they name: `dest_dev`: among the 256 pairs of one device no destination device is named more than 4 times, and in every draw some device names one destination exactly 4 times.
All inputs are finite; a program needn't handle non-finite values. No bound on the sum of `sea_mask` on one device may be relied on, other than what follows from the above.
Results may differ from a plain program's by a relative error of at most 0.0003.
Values sent between devices are 32-bit elements; how exact they have to be, the bound alone decides.
A program may use at most 128 MiB of HBM per device.

v0:
```python
import jax
import jax.numpy as jnp
from jax import lax
from jax.sharding import PartitionSpec as P

diffusion_rate = 0.2


def padded_2(cells, sides, width):
    for axis, dim in sides:
        count = lax.axis_size(axis)
        head = lax.slice_in_dim(cells, 0, width, axis=dim)
        tail = lax.slice_in_dim(cells, cells.shape[dim] - width, cells.shape[dim], axis=dim)
        cells = jnp.concatenate(
            [
                lax.ppermute(tail, axis, [(i, (i + 1) % count) for i in range(count)]),
                cells,
                lax.ppermute(head, axis, [((i + 1) % count, i) for i in range(count)]),
            ],
            axis=dim,
        )
    return cells


def on_device(
    atm_flux,
    sea_mask,
    src_block,
    dest_dev,
    dest_block,
    intersection_weights,
    coupling,
    inverses,
    ocean_state,
    depth_levels,
):
    lat_count = lax.axis_size("lat")
    blocks_dev = ocean_state.shape[2]
    depth_pad = padded_2(depth_levels, (("lat", 0), ("lon", 1)), 1)
    masked = atm_flux * sea_mask.astype(jnp.bfloat16)
    picked = jnp.take(masked, src_block, axis=1)
    contrib = jnp.einsum(
        "fka,kao->kfo", picked, intersection_weights, preferred_element_type=jnp.float32
    )
    tile_shape = contrib.shape[1:]
    destination = dest_dev[:, 0]
    target = destination * blocks_dev + dest_block
    inside = (target >= 0) & (target < blocks_dev * lax.axis_size(("lat", "lon")))
    placed = jnp.where(inside, target, blocks_dev * lax.axis_size(("lat", "lon")))
    received = lax.psum_scatter(
        jnp.zeros((blocks_dev * lax.axis_size(("lat", "lon")),) + tile_shape, jnp.float32)
        .at[placed]
        .add(contrib, mode="drop"),
        ("lat", "lon"),
        scatter_dimension=0,
        tiled=True,
    )
    forcing = jnp.einsum("qf,rfo->qro", coupling, received, precision=lax.Precision.HIGHEST)
    level_ids = jnp.arange(ocean_state.shape[1], dtype=jnp.int32)[:, None, None]
    active = level_ids < depth_levels[None]
    surface = ocean_state[:, 0] + forcing
    rhs = jnp.concatenate([surface[:, None], ocean_state[:, 1:]], axis=1)
    rhs = jnp.where(active[None], rhs, jnp.float32(0.0))
    solved = jnp.einsum("qrlm,qmrx->qlrx", inverses[:, :, 0], rhs, precision=lax.Precision.HIGHEST)
    mixed = jnp.where(active[None], solved, ocean_state)
    padded = padded_2(mixed, (("lat", 2), ("lon", 3)), 1)
    lat_here = lax.axis_index("lat")
    row_ids = jnp.arange(blocks_dev + 2, dtype=jnp.int32)
    band_edge = (row_ids == 0) & (lat_here == 0) | (row_ids == blocks_dev + 1) & (
        lat_here == lat_count - 1
    )
    depth_pad = jnp.where(band_edge[:, None], 0, depth_pad)
    active_pad = level_ids < depth_pad[None]
    neighbours = [
        (padded[:, :, 1:-1, 2:], active_pad[:, 1:-1, 2:]),
        (padded[:, :, 1:-1, :-2], active_pad[:, 1:-1, :-2]),
        (padded[:, :, 2:, 1:-1], active_pad[:, 2:, 1:-1]),
        (padded[:, :, :-2, 1:-1], active_pad[:, :-2, 1:-1]),
    ]
    total = jnp.zeros_like(mixed)
    for values, flags in neighbours:
        total = total + jnp.where(flags[None], values - mixed, jnp.float32(0.0))
    return mixed + diffusion_rate * jnp.where(active[None], total, jnp.float32(0.0))


def solution(mesh):
    placed = (
        P(None, "lat", "lon"),
        P("lat", "lon"),
        P(("lat", "lon")),
        P(("lat", "lon"), None),
        P(("lat", "lon")),
        P(("lat", "lon"), None, None),
        P(),
        P(None, "lat", "lon", None, None),
        P(None, None, "lat", "lon"),
        P("lat", "lon"),
    )
    return jax.shard_map(
        on_device,
        mesh=mesh,
        in_specs=placed,
        out_specs=P(None, None, "lat", "lon"),
        check_vma=False,
    )
```

profile of v0, /device:TPU:0, one launch (start us, length us, event | category | flops | bytes accessed | tf_op | source)
XLA Modules:
  0.0 788.6 jit_solution(4796702246440007420)
XLA Ops:
  6.5 0.7 compare_select_fusion
  7.2 0.7 compare_and_fusion
  7.9 0.8 convert_element_type.3
  8.7 0.7 broadcast_multiply_fusion
  9.4 1.0 copy_multiply_fusion
  10.4 0.8 gather_fusion
  11.2 0.7 compare_select_fusion.1
  11.9 4.7 fusion.24
  16.6 6.0 broadcast_in_dim.94
  22.6 25.2 %scatter_fusion = f32[4096,8,128]{2,1,0:T(8,128)} fusion(f32[4096,8,128]{2,1,0:T(8,128)} %broadcast_in_dim.94, s32[256]{0:T(256)S(1)} %compare_select_fusion.1, f32[256,8,128]{2,1,0:T(8,128)S(1)} %fusion.24), kind=kCustom, calls=%fused_computation.1 | custom fusion | flops 262144 | bytes 3146752 | tf_op jit(solution)/shard_map/scatter-add | solution.py:53
  47.8 0.7 copy-done.3
  48.5 1.9 collective-permute-start
  50.4 2.2 collective-permute-start.1
  52.8 1.3 collective-permute-done
  54.2 5.0 collective-permute-start.3
  59.3 5.4 copy.38
  64.8 651.6 %reduce-scatter.2.cloned.1.call-done = f32[32,8,128]{2,1,0:T(8,128)} async-done(((f32[4096,8,128]{2,1,0:T(8,128)}), f32[32,8,128]{2,1,0:T(8,128)}) %reduce-scatter.2.cloned.1.call-update) | async-done | bytes 131088 | tf_op jit(solution)/shard_map/reduce_scatter | solution.py:50
  716.4 1.2 fusion.23
  717.6 13.7 %bitcast_select_fusion = f32[4,80,32,128]{3,1,2,0:T(8,128)S(1)} fusion(pred[80,32,128]{2,0,1:T(8,128)(4,1)S(1)} %iota_compare_fusion.1, f32[4,32,1,80,80]{4,3,2,1,0:T(8,128)} %param.17, f32[4,79,32,128]{3,1,2,0:T(8,128)} %copy.38, f32[4,1,32,128]{3,1,2,0:T(1,128)S(1)} %copy.25, f32[4,80,32,128]{3,2,1,0:T(8,128)} %param.18), kind=kOutput, calls=%fused_computation.29 | convolution fusion | flops 1262223360 | bytes 19333120 | tf_op jit(solution)/shard_map/qrlm,qmrx->qlrx/dot_general | solution.py:64
  731.5 3.2 collective-permute-start.5
  735.1 2.9 collective-permute-done.4
  738.0 0.5 pad_maximum_fusion
  738.5 6.0 fusion.33
  744.5 3.5 copy.27
  748.1 3.5 copy.29
  751.7 0.6 collective-permute-start.7
  752.2 1.1 fusion.35
  753.4 3.4 copy.28
  756.7 2.1 collective-permute-done.7
  758.8 3.2 copy.30
  762.0 15.7 %fusion.5 = f32[4,80,32,128]{3,1,2,0:T(8,128)S(1)} fusion(f32[4,80,32,128]{3,1,2,0:T(8,128)} %copy-done.2, f32[4,80,1,128]{3,1,2,0:T(8,128)S(1)} %collective-permute-done.4, f32[4,80,1,128]{3,1,2,0:T(8,128)S(1)} %collective-permute-done.5, f32[4,80,34,1]{3,1,2,0:T(8,128)} %copy.30, f32[4,80,34,1]{3,1,2,0:T(8,128)} %copy.28, ...), kind=kLoop, calls=%fused_computation.9 | loop fusion | flops 28835840 | bytes 12538880 | tf_op jit(solution)/shard_map/add | solution.py:83
  777.8 4.0 copy.31
  (31 shorter events, 1.1 us)
Async XLA Ops:
  6.5 709.9 %copy-start = (f32[4,8]{1,0:T(4,128)S(1)}, f32[4,8]{1,0:T(4,128)}, u32[]{:S(2)}) copy-start(f32[4,8]{1,0:T(4,128)} %param.16) | copy-start | bytes 388
  6.5 709.9 %reduce-scatter.2.cloned.1.call-start = ((), (), s32[]{:S(2)}) async-start(), calls=%async_computation.1 | async-start | bytes 16908288 | tf_op jit(solution)/shard_map/reduce_scatter | solution.py:50
  47.8 0.7 copy-start.3
  48.5 5.6 collective-permute-start
  50.4 3.7 collective-permute-start.1
  52.8 6.5 slice-start.1
  54.2 10.4 %collective-permute-start.2 = (s32[34,1]{1,0:T(8,128)S(1)}, s32[34,1]{1,0:T(8,128)S(1)}, u32[]{:S(2)}, u32[]{:S(2)}) collective-permute-start(s32[34,1]{1,0:T(8,128)S(1)} %get-tuple-element.13), channel_id=1, source_target_pairs={{0,1},{1,2},{2,3},{3,4},{4,5},{5,6},{6,7},{7,8},{8,9},{9,10},{10,1... | collective-permute-start | bytes 416 | tf_op jit(solution)/shard_map/ppermute | solution.py:16
  54.2 662.2 %slice-start = ((f32[4,80,32,128]{3,2,1,0:T(8,128)}), f32[4,1,32,128]{3,2,1,0:T(8,128)S(1)}, s32[]{:S(2)}) async-start(f32[4,80,32,128]{3,2,1,0:T(8,128)} %param.18), calls=%async_computation.2 | async-start | bytes 131072 | tf_op jit(solution)/shard_map/slice | solution.py:61
  54.2 10.4 %collective-permute-start.3 = (s32[34,1]{1,0:T(8,128)S(1)}, s32[34,1]{1,0:T(8,128)S(1)}, u32[]{:S(2)}, u32[]{:S(2)}) collective-permute-start(s32[34,1]{1,0:T(8,128)S(1)} %get-tuple-element.14), channel_id=1, source_target_pairs={{1,0},{2,1},{3,2},{4,3},{5,4},{6,5},{7,6},{8,7},{9,8},{10,9},{11,1... | collective-permute-start | bytes 416 | tf_op jit(solution)/shard_map/ppermute | solution.py:18
  731.4 6.6 copy-start.2
  731.4 6.6 collective-permute-start.4
  731.5 6.5 collective-permute-start.5
  748.1 5.3 collective-permute-start.6
  751.7 7.1 collective-permute-start.7
  762.0 19.7 %copy-start.1 = (f32[4,8]{1,0:T(4,128)S(1)}, f32[4,8]{1,0:T(4,128)}, u32[]{:S(2)}) copy-start(f32[4,8]{1,0:T(4,128)} %param.16) | copy-start | bytes 388
Sparse Core Ops, SparseCore 0:
  47.9 668.4 reduce-scatter.1
where the time goes:
time: 790 us; the launch traced here: 789 us
  waiting for transfers between devices  658 us (83%)
  other arithmetic  46.5 us (6%)
  local copies, waits for them, and re-layouts  37.8 us (5%)
  matrix products  19.6 us (2%)
  between operations  13.6 us (2%)
  starting transfers between devices  13.1 us (2%)
    reduce_scatter x1, waiting for transfers between devices, on_device(): lax.psum_scatter(jnp.zeros((blocks_dev * lax.axis_size(('lat', 'lon')),)...  652 us
    scatter-add x1, other arithmetic, on_device(): received = lax.psum_scatter(jnp.zeros((blocks_dev * lax.axis_size(('lat',...  25.2 us
  transfers between devices with their start and end apart: 9, of which 4 were waited for; matrix products, arithmetic and copies ran while one was open for 2% of the time, Pallas kernels for 0%

commit v1 on v0

--- a/solution.py
+++ b/solution.py
@@ -1,9 +1,206 @@
+import functools
+
 import jax
 import jax.numpy as jnp
 from jax import lax
+from jax.experimental import pallas as pl
+from jax.experimental.pallas import tpu as pltpu
 from jax.sharding import PartitionSpec as P
 
 diffusion_rate = 0.2
+CAP = 4
+MESH = pl.DeviceIdType.MESH
+f32, bf16, i32 = jnp.float32, jnp.bfloat16, jnp.int32
+
+
+def halves(x):
+    high = x.astype(bf16)
+    return high, (x - high.astype(f32)).astype(bf16)
+
+
+def dot(a, b):
+    return jnp.dot(a, b, preferred_element_type=f32)
+
+
+def pack_kernel(
+    src_ref, coupling_ref, dest_ref, block_ref, atm_ref, mask_ref, weights_ref,
+    send_ref, meta_ref, table, contrib,
+):
+    step = pl.program_id(0)
+    pairs = weights_ref.shape[0]
+    fields, rows, cells = atm_ref.shape
+    total = dest_ref.shape[1]
+    devices = send_ref.shape[0]
+    q_count = coupling_ref.shape[0]
+
+    @pl.when(step == 0)
+    def _():
+        mask = mask_ref[...].astype(f32)
+        masked = [atm_ref[f].astype(f32) * mask for f in range(fields)]
+        for q in range(q_count):
+            row = masked[0] * coupling_ref[q, 0]
+            for f in range(1, fields):
+                row = row + masked[f] * coupling_ref[q, f]
+            high, low = halves(row)
+            table[pl.ds(q, rows, stride=8), :] = high.astype(f32)
+            table[pl.ds(q_count + q, rows, stride=8), :] = low.astype(f32)
+
+    def one(i, carry):
+        p = step * pairs + i
+        left = table[pl.ds(pl.multiple_of(src_ref[p] * 8, 8), 8), :].astype(bf16)
+        c = dot(left, weights_ref[i])
+        contrib[pl.ds(p, q_count, stride=total), :] = c[:q_count] + c[q_count:]
+        return carry
+
+    lax.fori_loop(0, pairs, one, 0, unroll=8)
+
+    @pl.when(step == pl.num_programs(0) - 1)
+    def _():
+        dest = dest_ref[...]
+        named = (lax.broadcasted_iota(i32, (devices, total), 0) == dest).astype(f32)
+        named_b = named.astype(bf16)
+        before = (
+            lax.broadcasted_iota(i32, (total, total), 0)
+            < lax.broadcasted_iota(i32, (total, total), 1)
+        ).astype(f32).astype(bf16)
+        rank = jnp.sum(named * dot(named_b, before), axis=0, keepdims=True).astype(i32)
+        lane = lax.broadcasted_iota(i32, (128, total), 0)
+        where_slot = (rank == lane % CAP).astype(f32) * block_ref[...].astype(f32)
+        blocks = lax.dot_general(
+            named_b, where_slot.astype(bf16), (((1,), (1,)), ((), ())),
+            preferred_element_type=f32,
+        )
+        me = lax.axis_index("lat") * lax.axis_size("lon") + lax.axis_index("lon")
+        lanes = lax.broadcasted_iota(i32, (devices, 128), 1)
+        key = blocks + ((lanes % 16) // CAP * 32).astype(f32)
+        meta_ref[...] = jnp.where(lanes // 16 == me % 8, key, 0.0)
+
+        slot = dest * 8 + rank
+        keys = jnp.concatenate([slot, slot + CAP], axis=1)
+        parts = []
+        for q2 in range(2):
+            parts.append(contrib[pl.ds(q2 * 2 * total, 2 * total), :])
+        high, low = halves(jnp.concatenate(parts, axis=1))
+        chunk = 256
+
+        def place(i, carry):
+            ids = lax.broadcasted_iota(i32, (chunk, 2 * total), 0) + i * chunk
+            hot = (ids == keys).astype(f32).astype(bf16)
+            out = dot(hot, high) + dot(hot, low)
+            for q2 in range(2):
+                send_ref[pl.ds(i * (chunk // 8), chunk // 8), pl.ds(q2 * 8, 8), :] = out[
+                    :, q2 * 128 : (q2 + 1) * 128
+                ].reshape(chunk // 8, 8, 128)
+            return carry
+
+        lax.fori_loop(0, devices * 8 // chunk, place, 0)
+
+
+def pack(src, coupling, dest, block, atm, mask, weights, devices):
+    pairs, cells, out_cells = weights.shape
+    group = 32
+    full = lambda shape: pl.BlockSpec(shape, lambda i: (0,) * len(shape))
+    return pl.pallas_call(
+        pack_kernel,
+        grid=(pairs // group,),
+        in_specs=[
+            pl.BlockSpec(memory_space=pltpu.SMEM),
+            pl.BlockSpec(memory_space=pltpu.SMEM),
+            full((1, pairs)),
+            full((1, pairs)),
+            full(atm.shape),
+            full(mask.shape),
+            pl.BlockSpec((group, cells, out_cells), lambda i: (i, 0, 0)),
+        ],
+        out_specs=[full((devices, 16, 128)), full((devices, 128))],
+        out_shape=[
+            jax.ShapeDtypeStruct((devices, 16, 128), f32),
+            jax.ShapeDtypeStruct((devices, 128), f32),
+        ],
+        scratch_shapes=[
+            pltpu.VMEM((8 * mask.shape[0], 128), f32),
+            pltpu.VMEM((4 * pairs, 128), f32),
+        ],
+        compiler_params=pltpu.CompilerParams(vmem_limit_bytes=32 << 20),
+        name="pack",
+    )(src, coupling, dest, block, atm, mask, weights)
+
+
+def exchange_kernel(n_lat, n_lon, send_ref, meta_ref, out_ref, recv, recv_meta, sems):
+    devices = n_lat * n_lon
+    lat, lon = lax.axis_index("lat"), lax.axis_index("lon")
+    me = lat * n_lon + lon
+    send_sem, recv_sem, send_meta_sem, recv_meta_sem = (sems.at[i] for i in range(4))
+
+    def peer(k):
+        core = (lon + k // 64) % 2
+        y = (lon // 2 + k // 4) % 4
+        x = (lon // 8 + k) % 4
+        z = (lat + k // 16) % 4
+        return z, (x * 4 + y) * 2 + core
+
+    barrier = pltpu.get_barrier_semaphore()
+
+    def greet(k, carry):
+        pl.semaphore_signal(barrier, inc=1, device_id=peer(k), device_id_type=MESH)
+        return carry
+
+    lax.fori_loop(1, devices, greet, 0)
+    pl.semaphore_wait(barrier, devices - 1)
+
+    def ship(k, carry):
+        z, o = peer(k)
+        to = z * n_lon + o
+        pltpu.make_async_remote_copy(
+            send_ref.at[to], recv.at[me], send_sem, recv_sem, device_id=(z, o), device_id_type=MESH
+        ).start()
+        pltpu.make_async_remote_copy(
+            meta_ref.at[to], recv_meta.at[me], send_meta_sem, recv_meta_sem,
+            device_id=(z, o), device_id_type=MESH,
+        ).start()
+        return carry
+
+    lax.fori_loop(1, devices, ship, 0)
+    pltpu.make_async_copy(send_ref.at[me], recv.at[me], recv_sem).start()
+    pltpu.make_async_copy(meta_ref.at[me], recv_meta.at[me], recv_meta_sem).start()
+    pltpu.make_async_copy(recv_meta, recv_meta, recv_meta_sem).wait()
+    pltpu.make_async_copy(recv, recv, recv_sem).wait()
+
+    out_ref[...] = jnp.zeros_like(out_ref)
+
+    def add(i, carry):
+        base = i * 16
+        keys = jnp.concatenate(
+            [jnp.sum(recv_meta[pl.ds(base + 8 * h, 8)], axis=0) for h in range(2)], axis=1
+        ).astype(i32)
+        hot = (lax.broadcasted_iota(i32, (128, 256), 0) == keys).astype(f32).astype(bf16)
+        high, low = halves(recv[pl.ds(base, 16)].reshape(256, 128))
+        out_ref[...] += dot(hot, high) + dot(hot, low)
+        return carry
+
+    lax.fori_loop(0, devices // 16, add, 0)
+    rest = pl.ds(0, devices - 1)
+    pltpu.make_async_copy(send_ref.at[rest], send_ref.at[rest], send_sem).wait()
+    pltpu.make_async_copy(meta_ref.at[rest], meta_ref.at[rest], send_meta_sem).wait()
+
+
+def exchange(send, meta, n_lat, n_lon):
+    devices = n_lat * n_lon
+    return pl.pallas_call(
+        functools.partial(exchange_kernel, n_lat, n_lon),
+        in_specs=[pl.BlockSpec(memory_space=pltpu.VMEM)] * 2,
+        out_specs=pl.BlockSpec(memory_space=pltpu.VMEM),
+        out_shape=jax.ShapeDtypeStruct((128, 128), f32),
+        scratch_shapes=[
+            pltpu.VMEM((devices, 16, 128), f32),
+            pltpu.VMEM((devices, 1, 128), f32),
+            pltpu.SemaphoreType.DMA((4,)),
+        ],
+        compiler_params=pltpu.CompilerParams(
+            collective_id=0, has_side_effects=True, vmem_limit_bytes=32 << 20
+        ),
+        name="exchange",
+    )(send, meta)
 
 
 def padded_2(cells, sides, width):
@@ -34,28 +231,17 @@
     ocean_state,
     depth_levels,
 ):
-    lat_count = lax.axis_size("lat")
+    n_lat, n_lon = lax.axis_size("lat"), lax.axis_size("lon")
+    lat_count = n_lat
     blocks_dev = ocean_state.shape[2]
+    pairs = src_block.shape[0]
+    send, meta = pack(
+        src_block, coupling, dest_dev.reshape(1, pairs), dest_block.reshape(1, pairs),
+        atm_flux, sea_mask, intersection_weights, n_lat * n_lon,
+    )
+    forcing = exchange(send, meta.reshape(n_lat * n_lon, 1, 128), n_lat, n_lon)
+    forcing = forcing.reshape(4, 32, 128)
     depth_pad = padded_2(depth_levels, (("lat", 0), ("lon", 1)), 1)
-    masked = atm_flux * sea_mask.astype(jnp.bfloat16)
-    picked = jnp.take(masked, src_block, axis=1)
-    contrib = jnp.einsum(
-        "fka,kao->kfo", picked, intersection_weights, preferred_element_type=jnp.float32
-    )
-    tile_shape = contrib.shape[1:]
-    destination = dest_dev[:, 0]
-    target = destination * blocks_dev + dest_block
-    inside = (target >= 0) & (target < blocks_dev * lax.axis_size(("lat", "lon")))
-    placed = jnp.where(inside, target, blocks_dev * lax.axis_size(("lat", "lon")))
-    received = lax.psum_scatter(
-        jnp.zeros((blocks_dev * lax.axis_size(("lat", "lon")),) + tile_shape, jnp.float32)
-        .at[placed]
-        .add(contrib, mode="drop"),
-        ("lat", "lon"),
-        scatter_dimension=0,
-        tiled=True,
-    )
-    forcing = jnp.einsum("qf,rfo->qro", coupling, received, precision=lax.Precision.HIGHEST)
     level_ids = jnp.arange(ocean_state.shape[1], dtype=jnp.int32)[:, None, None]
     active = level_ids < depth_levels[None]
     surface = ocean_state[:, 0] + forcing

time: 790 us -> 125 us (0.16)
  waiting for transfers between devices: 658 us -> 5.35 us
  Pallas kernels: 0 us -> 39.9 us
  other arithmetic: 46.5 us -> 18.7 us
  between operations: 13.6 us -> 0.29 us
  matrix products: 19.6 us -> 9.96 us
    reduce_scatter x1 -> x0, waiting for transfers between devices: 652 us -> none  [on_device(): lax.psum_scatter(jnp.zeros((blocks_dev * lax.axis_size(('lat', 'lon')),)...]
    pallas_call x0 -> x2, Pallas kernels: none -> 39.9 us  [the longest x1 31.6 us: exchange(): pl.pallas_call(functools.partial(exchange_kernel, n_lat, n_lon), in_specs...]
    scatter-add x1 -> x0, other arithmetic: 25.2 us -> none  [on_device(): received = lax.psum_scatter(jnp.zeros((blocks_dev * lax.axis_size(('lat',...]
  transfers between devices with their start and end apart: 9 -> 8, of which waited for: 4 -> 3; matrix products, arithmetic and copies ran while one was open for 2% -> 7% of each run, Pallas kernels for 0% -> 0%
where the time goes in v1:
time: 125 us
  Pallas kernels  39.9 us (32%)
  local copies, waits for them, and re-layouts  33.9 us (27%)
  other arithmetic  18.7 us (15%)
  starting transfers between devices  16.8 us (13%)
  matrix products  9.96 us (8%)
  waiting for transfers between devices  5.35 us (4%)
    pallas_call x1, Pallas kernels, exchange(): pl.pallas_call(functools.partial(exchange_kernel, n_lat, n_lon), in_specs...  31.6 us
    ppermute x4, starting transfers between devices, padded_2(): lax.ppermute(head, axis, [((i + 1) % count, i) for i in range(count)])  15.8 us
    add x1, other arithmetic, on_device(): mixed + diffusion_rate * jnp.where(active[None], total, jnp.float32(0.0))  15.1 us
    dot_general x1, matrix products, on_device(): jnp.einsum('qrlm,qmrx->qlrx', inverses[:, :, 0], rhs, precision=lax.Preci...  9.96 us
    slice x3, local copies, waits for them, and re-layouts, padded_2(): head = lax.slice_in_dim(cells, 0, width, axis=dim)  9.55 us
    unnamed x27, local copies, waits for them, and re-layouts  8.87 us
    pallas_call x1, Pallas kernels, pack(): pl.pallas_call(pack_kernel, grid=(pairs // group,), in_specs=[pl.BlockSpe...  8.39 us
    ppermute x4, waiting for transfers between devices, padded_2(): lax.ppermute(tail, axis, [(i, (i + 1) % count) for i in range(count)])  5.32 us
  transfers between devices with their start and end apart: 8, of which 3 were waited for; matrix products, arithmetic and copies ran while one was open for 7% of the time, Pallas kernels for 0%

profile of v1, /device:TPU:0, one launch (start us, length us, event | category | flops | bytes accessed | tf_op | source)
XLA Modules:
  0.0 125.0 jit_solution(13971560148147480211)
XLA Ops:
  0.1 0.6 copy-done.5
  0.7 0.2 copy-done.1
  0.9 2.6 %copy-done = bf16[256,128,128]{2,1,0:T(8,128)(2,1)S(1)} copy-done((bf16[256,128,128]{2,1,0:T(8,128)(2,1)S(1)}, bf16[256,128,128]{2,1,0:T(8,128)(2,1)}, u32[]{:S(2)}) %copy-start) | copy-done | bytes 8388632
  3.5 8.4 %pack.1 = (f32[128,16,128]{2,1,0:T(8,128)S(1)}, f32[128,128]{1,0:T(8,128)S(1)}) custom-call(s32[256]{0:T(256)S(1)} %copy-done.4, f32[4,8]{1,0:T(4,128)S(1)} %copy-done.3, s32[1,256]{1,0:T(1,128)S(1)} %bitcast.16, s32[1,256]{1,0:T(1,128)S(1)} %bitcast.17, bf16[8,64,128]{2,1,0:T(8,128)(2,1)S(1)} %copy-done.1, s32[64,128]{1,0:T(8,128)S(1)} %copy-done.2, ...), custom_call_target="tpu_custom_call" | custom-call | tf_op jit(solution)/shard_map/pack/pallas_call | solution.py:103
  11.9 31.6 %exchange.1 = f32[128,128]{1,0:T(8,128)S(1)} custom-call(f32[128,16,128]{2,1,0:T(8,128)S(1)} %get-tuple-element.7.send_ref, f32[128,1,128]{2,1,0:T(1,128)S(1)} %bitcast.15), custom_call_target="tpu_custom_call" | custom-call | tf_op jit(solution)/shard_map/exchange/pallas_call | solution.py:189
  43.6 0.2 iota_compare_fusion.1
  43.8 3.0 %copy.35 = f32[4,79,32,128]{3,1,2,0:T(8,128)S(1)} copy(f32[4,79,32,128]{3,2,1,0:T(8,128)S(1)} %slice-done.2) | data formatting | bytes 10354688
  46.8 10.0 %bitcast_select_fusion = f32[4,80,32,128]{3,1,2,0:T(8,128)S(1)} fusion(pred[80,32,128]{2,0,1:T(8,128)(4,1)S(1)} %iota_compare_fusion.1, f32[4,32,1,80,80]{4,3,2,1,0:T(8,128)S(1)} %bitcast.21, f32[4,79,32,128]{3,1,2,0:T(8,128)S(1)} %copy.35, f32[4,1,32,128]{3,1,2,0:T(1,128)S(1)} %bitcast.22, f32[4,80,32,128]{3,2,1,0:T(8,128)S(1)} %bitcast.19), kind=kOutput, calls=%fused_computation.27 | convolution fusion | flops 1262223360 | bytes 19333120 | tf_op jit(solution)/shard_map/qrlm,qmrx->qlrx/dot_general | solution.py:250
  56.8 2.3 %copy-done.7 = f32[4,80,32,128]{3,1,2,0:T(8,128)} copy-done((f32[4,80,32,128]{3,1,2,0:T(8,128)}, f32[4,80,32,128]{3,1,2,0:T(8,128)S(1)}, u32[]{:S(2)}) %copy-start.7) | copy-done | bytes 5242904
  59.2 0.9 collective-permute-start.4
  60.1 2.4 %collective-permute-start.5 = (f32[4,80,1,128]{3,1,2,0:T(8,128)S(1)}, f32[4,80,1,128]{3,1,2,0:T(8,128)S(1)}, u32[]{:S(2)}, u32[]{:S(2)}) collective-permute-start(f32[4,80,1,128]{3,1,2,0:T(8,128)S(1)} %get-tuple-element.11), channel_id=1, source_target_pairs={{32,0},{64,32},{96,64},{0,96},{33,1},{65,33},{97,65},{1,97},{34,2}... | collective-permute-start | bytes 491528 | tf_op jit(solution)/shard_map/ppermute | solution.py:215
  62.5 3.2 %collective-permute-start.1 = (s32[1,128]{1,0:T(1,128)S(1)}, s32[1,128]{1,0:T(1,128)S(1)}, u32[]{:S(2)}, u32[]{:S(2)}) collective-permute-start(s32[1,128]{1,0:T(1,128)S(1)} %get-tuple-element.20), channel_id=1, source_target_pairs={{32,0},{64,32},{96,64},{0,96},{33,1},{65,33},{97,65},{1,97},{34,2}... | collective-permute-start | bytes 1544 | tf_op jit(solution)/shard_map/ppermute | solution.py:215
  65.7 1.5 %collective-permute-done = s32[1,128]{1,0:T(1,128)S(1)} collective-permute-done((s32[1,128]{1,0:T(1,128)S(1)}, s32[1,128]{1,0:T(1,128)S(1)}, u32[]{:S(2)}, u32[]{:S(2)}) %collective-permute-start) | collective-permute-done | bytes 544 | tf_op jit(solution)/shard_map/ppermute | solution.py:213
  67.3 0.1 fusion.27
  67.3 0.0 collective-permute-start.2
  67.4 5.1 %collective-permute-start.3 = (s32[34,1]{1,0:T(8,128)S(1)}, s32[34,1]{1,0:T(8,128)S(1)}, u32[]{:S(2)}, u32[]{:S(2)}) collective-permute-start(s32[34,1]{1,0:T(8,128)S(1)} %get-tuple-element.18), channel_id=1, source_target_pairs={{1,0},{2,1},{3,2},{4,3},{5,4},{6,5},{7,6},{8,7},{9,8},{10,9},{11,1... | collective-permute-start | bytes 416 | tf_op jit(solution)/shard_map/ppermute | solution.py:215
  72.4 1.5 %collective-permute-done.2 = s32[34,1]{1,0:T(8,128)S(1)} collective-permute-done((s32[34,1]{1,0:T(8,128)S(1)}, s32[34,1]{1,0:T(8,128)S(1)}, u32[]{:S(2)}, u32[]{:S(2)}) %collective-permute-start.2) | collective-permute-done | bytes 168 | tf_op jit(solution)/shard_map/ppermute | solution.py:213
  73.9 0.0 collective-permute-done.3
  73.9 0.1 add_select_fusion
  74.0 0.4 iota_compare_fusion
  74.4 2.9 %pad_maximum_fusion = f32[4,80,34,128]{3,1,2,0:T(8,128)S(1)} fusion(f32[4,80,1,128]{3,1,2,0:T(8,128)S(1)} %collective-permute-done.5, f32[4,80,32,128]{3,1,2,0:T(8,128)} %copy-done.7, f32[4,80,1,128]{3,1,2,0:T(8,128)S(1)} %collective-permute-done.4), kind=kLoop, calls=%fused_computation | loop fusion | flops 2785280 | bytes 11141120 | tf_op jit(solution)/shard_map/concatenate | solution.py:211
  77.3 6.0 %fusion.24 = (f32[4,80,34,1]{3,1,2,0:T(8,128)}, f32[4,80,34,1]{3,1,2,0:T(8,128)}) fusion(f32[4,80,34,128]{3,1,2,0:T(8,128)S(1)} %pad_maximum_fusion), kind=kLoop, calls=%fused_computation.39 | loop fusion | bytes 174080 | tf_op jit(solution)/shard_map/slice | solution.py:209
  83.3 3.5 %copy.29 = f32[4,80,34,1]{1,0,3,2:T(4,128)S(1)} copy(f32[4,80,34,1]{3,1,2,0:T(8,128)} %get-tuple-element.9) | data formatting | bytes 87040 | tf_op jit(solution)/shard_map/slice | solution.py:209
  86.8 5.1 %collective-permute-start.6 = (f32[4,80,34,1]{1,0,3,2:T(4,128)S(1)}, f32[4,80,34,1]{1,0,3,2:T(4,128)S(1)}, u32[]{:S(2)}, u32[]{:S(2)}) collective-permute-start(f32[4,80,34,1]{1,0,3,2:T(4,128)S(1)} %copy.29), channel_id=1, source_target_pairs={{1,0},{2,1},{3,2},{4,3},{5,4},{6,5},{7,6},{8,7},{9,8},{10,9},{11,1... | collective-permute-start | bytes 130568 | tf_op jit(solution)/shard_map/ppermute | solution.py:215
  92.0 3.5 %copy.31 = f32[4,80,34,1]{1,0,3,2:T(4,128)S(1)} copy(f32[4,80,34,1]{3,1,2,0:T(8,128)} %get-tuple-element.10) | data formatting | bytes 87040 | tf_op jit(solution)/shard_map/slice | solution.py:210
  95.5 0.1 collective-permute-start.7
  95.6 1.1 fusion.26
  96.7 3.5 %copy.30 = f32[4,80,34,1]{3,1,2,0:T(8,128)} copy(f32[4,80,34,1]{1,0,3,2:T(4,128)S(1)} %collective-permute-done.6) | data formatting | bytes 87040 | tf_op jit(solution)/shard_map/ppermute | solution.py:215
  100.3 2.4 %collective-permute-done.7 = f32[4,80,34,1]{1,0,3,2:T(4,128)S(1)} collective-permute-done((f32[4,80,34,1]{1,0,3,2:T(4,128)S(1)}, f32[4,80,34,1]{1,0,3,2:T(4,128)S(1)}, u32[]{:S(2)}, u32[]{:S(2)}) %collective-permute-start.7) | collective-permute-done | bytes 43552 | tf_op jit(solution)/shard_map/ppermute | solution.py:213
  102.6 3.3 %copy.32 = f32[4,80,34,1]{3,1,2,0:T(8,128)} copy(f32[4,80,34,1]{1,0,3,2:T(4,128)S(1)} %collective-permute-done.7) | data formatting | bytes 87040 | tf_op jit(solution)/shard_map/ppermute | solution.py:213
  105.9 15.1 %fusion.5 = f32[4,80,32,128]{3,1,2,0:T(8,128)S(1)} fusion(f32[4,80,32,128]{3,1,2,0:T(8,128)} %copy-done.7, f32[4,80,1,128]{3,1,2,0:T(8,128)S(1)} %collective-permute-done.4, f32[4,80,1,128]{3,1,2,0:T(8,128)S(1)} %collective-permute-done.5, f32[4,80,34,1]{3,1,2,0:T(8,128)} %copy.32, f32[4,80,34,1]{3,1,2,0:T(8,128)} %copy.30, ...), kind=kLoop, calls=%fused_computation.7 | loop fusion | flops 28835840 | bytes 12538880 | tf_op jit(solution)/shard_map/add | solution.py:269
  121.0 4.0 %copy.33 = f32[4,80,32,128]{3,2,1,0:T(8,128)} copy(f32[4,80,32,128]{3,1,2,0:T(8,128)S(1)} %fusion.5) | data formatting | bytes 10485760 | tf_op jit(solution)/shard_map/add | solution.py:269
  (36 shorter events, 0.1 us)
Async XLA Ops:
  0.0 0.7 copy-start.5
  0.0 0.7 copy-start.6
  0.0 0.9 copy-start.1
  0.0 0.9 copy-start.2
  0.0 0.9 copy-start.4
  0.0 3.5 %copy-start = (bf16[256,128,128]{2,1,0:T(8,128)(2,1)S(1)}, bf16[256,128,128]{2,1,0:T(8,128)(2,1)}, u32[]{:S(2)}) copy-start(bf16[256,128,128]{2,1,0:T(8,128)(2,1)} %weights_ref.1) | copy-start | bytes 25165828
  0.0 3.5 %copy-start.3 = (f32[4,8]{1,0:T(4,128)S(1)}, f32[4,8]{1,0:T(4,128)}, u32[]{:S(2)}) copy-start(f32[4,8]{1,0:T(4,128)} %coupling_ref.1) | copy-start | bytes 388
  0.0 43.7 %slice-start.2 = ((f32[4,80,32,128]{3,2,1,0:T(8,128)}), f32[4,79,32,128]{3,2,1,0:T(8,128)S(1)}, s32[]{:S(2)}) async-start(f32[4,80,32,128]{3,2,1,0:T(8,128)} %param.18), calls=%async_computation.2 | async-start | bytes 10354688 | tf_op jit(solution)/shard_map/slice | solution.py:248
  0.0 43.5 %slice-start = ((s8[5242880]{0:T(1024)(128)(4,1)}), s8[4194304]{0:T(1024)(128)(4,1)S(1)}, s32[]{:S(2)}) async-start(s8[5242880]{0:T(1024)(128)(4,1)} %bitcast.18), calls=%async_computation | async-start | bytes 8388608
  0.1 43.5 %copy-start.8 = (s32[32,128]{1,0:T(8,128)S(1)}, s32[32,128]{1,0:T(8,128)}, u32[]{:S(2)}) copy-start(s32[32,128]{1,0:T(8,128)} %param.19) | copy-start | bytes 49156
  3.5 40.0 %slice-start.1 = ((s8[5242880]{0:T(1024)(128)(4,1)}), s8[1048576]{0:T(1024)(128)(4,1)S(1)}, s32[]{:S(2)}) async-start(s8[5242880]{0:T(1024)(128)(4,1)} %bitcast.18), calls=%async_computation.1 | async-start | bytes 2097152
  43.6 3.2 %slice-start.3 = ((s8[5242880]{0:T(1024)(128)(4,1)}), s8[4194304]{0:T(1024)(128)(4,1)S(1)}, s32[]{:S(2)}) async-start(s8[5242880]{0:T(1024)(128)(4,1)} %bitcast.20), calls=%async_computation.3 | async-start | bytes 8388608
  43.8 3.0 %slice-start.4 = ((s8[5242880]{0:T(1024)(128)(4,1)}), s8[1048576]{0:T(1024)(128)(4,1)S(1)}, s32[]{:S(2)}) async-start(s8[5242880]{0:T(1024)(128)(4,1)} %bitcast.20), calls=%async_computation.4 | async-start | bytes 2097152
  56.8 2.4 %copy-start.7 = (f32[4,80,32,128]{3,1,2,0:T(8,128)}, f32[4,80,32,128]{3,1,2,0:T(8,128)S(1)}, u32[]{:S(2)}) copy-start(f32[4,80,32,128]{3,1,2,0:T(8,128)S(1)} %bitcast_select_fusion) | copy-start | bytes 15728644
  59.2 15.2 %collective-permute-start.4 = (f32[4,80,1,128]{3,1,2,0:T(8,128)S(1)}, f32[4,80,1,128]{3,1,2,0:T(8,128)S(1)}, u32[]{:S(2)}, u32[]{:S(2)}) collective-permute-start(f32[4,80,1,128]{3,1,2,0:T(8,128)S(1)} %get-tuple-element.12), channel_id=1, source_target_pairs={{0,32},{32,64},{64,96},{96,0},{1,33},{33,65},{65,97},{97,1},{2,34}... | collective-permute-start | bytes 491528 | tf_op jit(solution)/shard_map/ppermute | solution.py:213
  60.1 14.3 %collective-permute-start.5 = (f32[4,80,1,128]{3,1,2,0:T(8,128)S(1)}, f32[4,80,1,128]{3,1,2,0:T(8,128)S(1)}, u32[]{:S(2)}, u32[]{:S(2)}) collective-permute-start(f32[4,80,1,128]{3,1,2,0:T(8,128)S(1)} %get-tuple-element.11), channel_id=1, source_target_pairs={{32,0},{64,32},{96,64},{0,96},{33,1},{65,33},{97,65},{1,97},{34,2}... | collective-permute-start | bytes 491528 | tf_op jit(solution)/shard_map/ppermute | solution.py:215
  62.5 4.8 %collective-permute-start = (s32[1,128]{1,0:T(1,128)S(1)}, s32[1,128]{1,0:T(1,128)S(1)}, u32[]{:S(2)}, u32[]{:S(2)}) collective-permute-start(s32[1,128]{1,0:T(1,128)S(1)} %get-tuple-element.19), channel_id=1, source_target_pairs={{0,32},{32,64},{64,96},{96,0},{1,33},{33,65},{65,97},{97,1},{2,34}... | collective-permute-start | bytes 1544 | tf_op jit(solution)/shard_map/ppermute | solution.py:213
  62.5 4.8 %collective-permute-start.1 = (s32[1,128]{1,0:T(1,128)S(1)}, s32[1,128]{1,0:T(1,128)S(1)}, u32[]{:S(2)}, u32[]{:S(2)}) collective-permute-start(s32[1,128]{1,0:T(1,128)S(1)} %get-tuple-element.20), channel_id=1, source_target_pairs={{32,0},{64,32},{96,64},{0,96},{33,1},{65,33},{97,65},{1,97},{34,2}... | collective-permute-start | bytes 1544 | tf_op jit(solution)/shard_map/ppermute | solution.py:215
  67.3 6.5 %collective-permute-start.2 = (s32[34,1]{1,0:T(8,128)S(1)}, s32[34,1]{1,0:T(8,128)S(1)}, u32[]{:S(2)}, u32[]{:S(2)}) collective-permute-start(s32[34,1]{1,0:T(8,128)S(1)} %get-tuple-element.17), channel_id=1, source_target_pairs={{0,1},{1,2},{2,3},{3,4},{4,5},{5,6},{6,7},{7,8},{8,9},{9,10},{10,1... | collective-permute-start | bytes 416 | tf_op jit(solution)/shard_map/ppermute | solution.py:213
  67.4 6.5 %collective-permute-start.3 = (s32[34,1]{1,0:T(8,128)S(1)}, s32[34,1]{1,0:T(8,128)S(1)}, u32[]{:S(2)}, u32[]{:S(2)}) collective-permute-start(s32[34,1]{1,0:T(8,128)S(1)} %get-tuple-element.18), channel_id=1, source_target_pairs={{1,0},{2,1},{3,2},{4,3},{5,4},{6,5},{7,6},{8,7},{9,8},{10,9},{11,1... | collective-permute-start | bytes 416 | tf_op jit(solution)/shard_map/ppermute | solution.py:215
  86.8 9.8 %collective-permute-start.6 = (f32[4,80,34,1]{1,0,3,2:T(4,128)S(1)}, f32[4,80,34,1]{1,0,3,2:T(4,128)S(1)}, u32[]{:S(2)}, u32[]{:S(2)}) collective-permute-start(f32[4,80,34,1]{1,0,3,2:T(4,128)S(1)} %copy.29), channel_id=1, source_target_pairs={{1,0},{2,1},{3,2},{4,3},{5,4},{6,5},{7,6},{8,7},{9,8},{10,9},{11,1... | collective-permute-start | bytes 130568 | tf_op jit(solution)/shard_map/ppermute | solution.py:215
  95.5 7.1 %collective-permute-start.7 = (f32[4,80,34,1]{1,0,3,2:T(4,128)S(1)}, f32[4,80,34,1]{1,0,3,2:T(4,128)S(1)}, u32[]{:S(2)}, u32[]{:S(2)}) collective-permute-start(f32[4,80,34,1]{1,0,3,2:T(4,128)S(1)} %copy.31), channel_id=1, source_target_pairs={{0,1},{1,2},{2,3},{3,4},{4,5},{5,6},{6,7},{7,8},{8,9},{9,10},{10,1... | collective-permute-start | bytes 130568 | tf_op jit(solution)/shard_map/ppermute | solution.py:213

commit v2 on v0

v2 whole, which is shorter than its diff:
```python
import functools

import jax
import jax.numpy as jnp
from jax import lax
from jax.experimental import pallas as pl
from jax.experimental.pallas import tpu as pltpu
from jax.sharding import PartitionSpec as P

diffusion_rate = 0.2
CAP = 4
MESH = pl.DeviceIdType.MESH
NORTH, SOUTH, WEST, EAST = range(4)
f32, bf16, i32 = jnp.float32, jnp.bfloat16, jnp.int32
VMEM_BYTES = 62 << 20


def halves(x):
    high = x.astype(bf16)
    return high, (x - high.astype(f32)).astype(bf16)


def dot(a, b):
    return jnp.dot(a, b, preferred_element_type=f32)


def iota(shape, dim):
    return lax.broadcasted_iota(i32, shape, dim)


def one_hot(flags):
    return flags.astype(f32).astype(bf16)


def couple_kernel(
    n_lat, n_lon,
    src_ref, coupling_ref, dest_ref, block_ref, atm_ref, mask_ref, depth_ref,
    weights_hbm, inverses_hbm, ocean_hbm,
    base_hbm, force_ref, gain_ref, rows_ref, cols_ref, sides_ref,
    weights, inverses, ocean, base, table, contrib,
    send, meta, recv, recv_meta, partial, partial_in,
    col_out, gain_t, gain_out, force_out, strip_out,
    row_in, col_in, gain_in, gain_strip_in, depth_in, force_in, strip_in,
    load_sems, ship_sems, halo_send, halo_recv, force_send, force_recv,
):
    chips = n_lat * n_lon // 2
    devices = 2 * chips
    lat, lon = lax.axis_index("lat"), lax.axis_index("lon")
    core = lon % 2
    my_chip = lat * (n_lon // 2) + lon // 2
    q_count = coupling_ref.shape[0]
    pairs = dest_ref.shape[1]
    levels = inverses.shape[2]
    o_rows = depth_ref.shape[0]

    w_chunks = 8
    w_size = pairs // w_chunks

    def weight_copy(c):
        part = pl.ds(c * w_size, w_size)
        return pltpu.make_async_copy(weights_hbm.at[part], weights.at[part], load_sems.at[c])

    for c in range(w_chunks):
        weight_copy(c).start()
    inverse_copy = pltpu.make_async_copy(inverses_hbm, inverses, load_sems.at[w_chunks])
    ocean_copy = pltpu.make_async_copy(ocean_hbm, ocean, load_sems.at[w_chunks + 1])
    inverse_copy.start()
    ocean_copy.start()

    barrier = pltpu.get_barrier_semaphore()

    def peer(k):
        x = (lon // 8 + k) % 4
        y = (lon // 2 + k // 4) % 4
        z = (lat + k // 16) % 4
        return z, (x * 4 + y) * 2 + core

    beside = {
        NORTH: ((lat + n_lat - 1) % n_lat, lon),
        SOUTH: ((lat + 1) % n_lat, lon),
        WEST: (lat, (lon + n_lon - 1) % n_lon),
        EAST: (lat, (lon + 1) % n_lon),
    }
    partner = (lat, lon + 1 - 2 * core)

    def greet(k, carry):
        pl.semaphore_signal(barrier, inc=1, device_id=peer(k), device_id_type=MESH)
        return carry

    lax.fori_loop(1, chips, greet, 0)
    for side in (WEST, EAST):
        pl.semaphore_signal(barrier, inc=1, device_id=beside[side], device_id_type=MESH)

    a_rows = mask_ref.shape[0]
    mask = mask_ref[...].astype(f32)
    masked = [atm_ref[f].astype(f32) * mask for f in range(atm_ref.shape[0])]
    for q in range(q_count):
        row = masked[0] * coupling_ref[q, 0]
        for f in range(1, atm_ref.shape[0]):
            row = row + masked[f] * coupling_ref[q, f]
        high, low = halves(row)
        contrib[pl.ds(q, a_rows, stride=8), :] = high.astype(f32)
        contrib[pl.ds(q_count + q, a_rows, stride=8), :] = low.astype(f32)
    table[...] = contrib[pl.ds(0, 8 * a_rows), :].reshape(a_rows, 8, 128)

    dest = dest_ref[...]
    named = (iota((devices, pairs), 0) == dest).astype(f32)
    before = one_hot(iota((pairs, pairs), 0) < iota((pairs, pairs), 1))
    rank = jnp.sum(named * dot(named.astype(bf16), before), axis=0, keepdims=True).astype(i32)
    lane = iota((128, pairs), 0)
    of_chip = one_hot(iota((chips, pairs), 0) == dest // 2)
    held = ((rank == lane % CAP) & (dest % 2 == lane % 32 // 16)).astype(f32)
    held = (held * block_ref[...].astype(f32)).astype(bf16)
    blocks = lax.dot_general(of_chip, held, (((1,), (1,)), ((), ())), preferred_element_type=f32)
    lanes = iota((chips, 128), 1)
    key = blocks + (lanes % 32 // 16 * 128 + lanes % 16 // CAP * o_rows).astype(f32)
    key = jnp.where(lanes // 32 == my_chip % 4, key, 0.0)
    for h in range(chips):
        meta[h] = key[h : h + 1]
    slot = dest * 8 + rank
    keys = jnp.concatenate([slot, slot + CAP], axis=1)

    def chunk_of_pairs(c, carry):
        weight_copy(c).wait()

        def four(i, carry):
            p = c * w_size + i * 4
            lefts = []
            for j in range(4):
                left = table[src_ref[p + j]]
                zero = jnp.zeros_like(left)
                lefts.append(jnp.concatenate([left, zero] if j % 2 == 0 else [zero, left], axis=1))
            left = jnp.concatenate(lefts, axis=0).astype(bf16)
            w = [weights[p + j] for j in range(4)]
            right = jnp.concatenate(
                [jnp.concatenate(w[:2], axis=0), jnp.concatenate(w[2:], axis=0)], axis=1
            )
            out = dot(left, right)
            for j in range(4):
                both = out[j * 8 : j * 8 + 8, j // 2 * 128 : j // 2 * 128 + 128]
                contrib[pl.ds(p + j, q_count, stride=pairs), :] = both[:q_count] + both[q_count:]
            return carry

        return lax.fori_loop(0, w_size // 4, four, carry, unroll=4)

    lax.fori_loop(0, w_chunks, chunk_of_pairs, 0)

    high, low = halves(
        jnp.concatenate(
            [contrib[pl.ds(h * 2 * pairs, 2 * pairs), :] for h in range(2)], axis=1
        )
    )
    chunk = 256

    def place(i, carry):
        hot = one_hot(iota((chunk, 2 * pairs), 0) + i * chunk == keys)
        out = dot(hot, high) + dot(hot, low)
        for h in range(2):
            send[pl.ds(i * (chunk // 8), chunk // 8), pl.ds(h * 8, 8), :] = out[
                :, h * 128 : (h + 1) * 128
            ].reshape(chunk // 8, 8, 128)
        return carry

    lax.fori_loop(0, devices * 8 // chunk, place, 0)

    pl.semaphore_wait(barrier, chips + 1)
    send_sem, recv_sem, meta_send_sem, meta_recv_sem = (ship_sems.at[i] for i in range(4))

    def ship(k, carry):
        z, o = peer(k)
        to = z * (n_lon // 2) + o // 2
        pltpu.make_async_remote_copy(
            send.at[pl.ds(2 * to, 2)], recv.at[pl.ds(2 * my_chip, 2)], send_sem, recv_sem,
            device_id=(z, o), device_id_type=MESH,
        ).start()
        pltpu.make_async_remote_copy(
            meta.at[to], recv_meta.at[my_chip], meta_send_sem, meta_recv_sem,
            device_id=(z, o), device_id_type=MESH,
        ).start()
        return carry

    lax.fori_loop(1, chips, ship, 0)
    mine = pl.ds(2 * my_chip, 2)
    pltpu.make_async_copy(send.at[mine], recv.at[mine], recv_sem).start()
    pltpu.make_async_copy(meta.at[my_chip], recv_meta.at[my_chip], meta_recv_sem).start()

    inverse_copy.wait()
    ocean_copy.wait()
    gain_ref[...] = jnp.zeros_like(gain_ref)
    level = iota((levels, 128), 0)
    lane_id = iota((levels, 128), 1)

    def mix(i, carry):
        q, r = i // o_rows, i % o_rows
        state = ocean[pl.ds(q * levels * o_rows + r, levels, stride=o_rows), :]
        active = level < depth_ref[pl.ds(r, 1), :]
        inverse = inverses[q, r]
        left = jnp.concatenate(halves(inverse), axis=0)
        right = jnp.concatenate(halves(jnp.where(active, state, 0.0)), axis=1)
        out = dot(left, right)
        solved = out[:levels, :128] + (out[:levels, 128:] + out[levels:, :128])
        mixed = jnp.where(active, solved, state)
        base[q, r] = mixed
        here = lane_id == i
        col_out[0] = jnp.where(here, jnp.broadcast_to(mixed[:, :1], mixed.shape), col_out[0])
        col_out[1] = jnp.where(here, jnp.broadcast_to(mixed[:, 127:], mixed.shape), col_out[1])
        gain_ref[pl.ds(0, levels), :] = jnp.where(
            here, jnp.broadcast_to(inverse[:, :1], mixed.shape), gain_ref[pl.ds(0, levels), :]
        )
        return carry

    lax.fori_loop(0, q_count * o_rows, mix, 0, unroll=2)
    base_copy = pltpu.make_async_copy(base, base_hbm, load_sems.at[w_chunks + 2])
    base_copy.start()
    gain_t[...] = jnp.transpose(gain_ref[...])
    for s, r in ((0, 0), (1, o_rows - 1)):
        gain_out[s, pl.ds(0, q_count), :] = gain_t[pl.ds(r, q_count, stride=o_rows), :]

    copies = []

    def hand(side, source, target):
        opposite = (SOUTH, NORTH, EAST, WEST)[side]
        n = len(copies)
        copy = pltpu.make_async_remote_copy(
            source, target(opposite), halo_send.at[n], halo_recv.at[n],
            device_id=beside[side], device_id_type=MESH,
        )
        copy.start()
        copies.append(copy)

    for side, r in ((NORTH, 0), (SOUTH, o_rows - 1)):
        hand(side, base.at[:, r], lambda o: row_in.at[o])
        hand(side, gain_out.at[side], lambda o: gain_strip_in.at[o])
    for side in (WEST, EAST):
        hand(side, col_out.at[side - 2], lambda o: col_in.at[o - 2])
        hand(side, gain_ref.at[pl.ds(0, levels)], lambda o: gain_in.at[o - 2])
    for side in range(4):
        hand(side, depth_ref, lambda o: depth_in.at[o])
    for copy in copies:
        copy.wait()

    every = pl.ds(0, chips)
    pltpu.make_async_copy(recv_meta, recv_meta, meta_recv_sem).wait()
    pltpu.make_async_copy(recv, recv, recv_sem).wait()
    partial[...] = jnp.zeros_like(partial)

    def add(i, carry):
        at = i * 8
        keys = jnp.concatenate(
            [jnp.sum(recv_meta[pl.ds(at + 4 * h, 4)], axis=0) for h in range(2)], axis=1
        ).astype(i32)
        hot = one_hot(iota((256, 256), 0) == keys)
        high, low = halves(recv[pl.ds(2 * at, 16)].reshape(256, 128))
        partial[...] += (dot(hot, high) + dot(hot, low)).reshape(2, 128, 128)
        return carry

    lax.fori_loop(0, chips // 8, add, 0)
    swap = pltpu.make_async_remote_copy(
        partial.at[1 - core], partial_in, force_send.at[4], force_recv.at[4],
        device_id=partner, device_id_type=MESH,
    )
    swap.start()
    swap.wait()
    force = partial[core] + partial_in[...]
    force_ref[...] = force
    for s, r in ((0, 0), (1, o_rows - 1)):
        force_out[s, pl.ds(0, q_count), :] = force_ref[pl.ds(r, q_count, stride=o_rows), :]
    force_t = jnp.transpose(force)
    strip_out[0, pl.ds(0, 1), :] = force_t[:1]
    strip_out[1, pl.ds(0, 1), :] = force_t[127:]
    forces = []
    for side in range(4):
        opposite = (SOUTH, NORTH, EAST, WEST)[side]
        out, into = (force_out, force_in) if side < 2 else (strip_out, strip_in)
        copy = pltpu.make_async_remote_copy(
            out.at[side % 2], into.at[opposite % 2], force_send.at[side], force_recv.at[side],
            device_id=beside[side], device_id_type=MESH,
        )
        copy.start()
        forces.append(copy)

    depth = depth_ref[...]
    in_band = (lat > 0).astype(i32), (lat < n_lat - 1).astype(i32)
    north_depth = depth_in[NORTH] * in_band[0]
    south_depth = depth_in[SOUTH] * in_band[1]
    row_id, cell_id = iota(depth.shape, 0), iota(depth.shape, 1)
    roll = pltpu.roll
    sides_ref[NORTH] = jnp.where(row_id == 0, roll(north_depth, 1, 0), roll(depth, 1, 0))
    sides_ref[SOUTH] = jnp.where(
        row_id == o_rows - 1, roll(south_depth, o_rows - 1, 0), roll(depth, o_rows - 1, 0)
    )
    sides_ref[WEST] = jnp.where(cell_id == 0, roll(depth_in[WEST], 1, 1), roll(depth, 1, 1))
    sides_ref[EAST] = jnp.where(cell_id == 127, roll(depth_in[EAST], 127, 1), roll(depth, 127, 1))
    turned = [
        jnp.transpose(jnp.concatenate([depth_in[s].astype(f32)] * q_count, axis=0))
        for s in (WEST, EAST)
    ]
    limits = turned[0][127:].astype(i32), turned[1][:1].astype(i32)
    strips = jnp.transpose(
        jnp.concatenate(
            [gain_strip_in[0], gain_strip_in[1], jnp.zeros((112, 128), f32)], axis=0
        )
    )
    for copy in forces:
        copy.wait()
    edges = north_depth[o_rows - 1 :], south_depth[:1]
    for s in range(2):
        for q in range(q_count):
            gain = jnp.broadcast_to(strips[:levels, s * 8 + q : s * 8 + q + 1], (levels, 128))
            value = row_in[s, q] + gain * force_in[s, pl.ds(q, 1), :]
            rows_ref[s, q] = jnp.where(level < edges[s], value, 0.0)
        value = col_in[s] + gain_in[s] * strip_in[s, pl.ds(0, 1), :]
        cols_ref[s] = jnp.where(level < limits[s], value, 0.0)

    rest = pl.ds(0, 2 * (chips - 1))
    pltpu.make_async_copy(send.at[rest], send.at[rest], send_sem).wait()
    rest = pl.ds(0, chips - 1)
    pltpu.make_async_copy(meta.at[rest], meta.at[rest], meta_send_sem).wait()
    base_copy.wait()


def couple(src, coupling, dest, block, atm, mask, depth, weights, inverses, ocean, n_lat, n_lon):
    pairs = src.shape[0]
    q_count, o_rows, levels, _ = inverses.shape
    chips = n_lat * n_lon // 2
    vmem, smem, hbm = (
        pl.BlockSpec(memory_space=s) for s in (pltpu.VMEM, pltpu.SMEM, pl.ANY)
    )
    shape = jax.ShapeDtypeStruct
    V, DMA = pltpu.VMEM, pltpu.SemaphoreType.DMA
    return pl.pallas_call(
        functools.partial(couple_kernel, n_lat, n_lon),
        in_specs=[smem, smem] + [vmem] * 5 + [hbm] * 3,
        out_specs=[hbm] + [vmem] * 5,
        out_shape=[
            shape((q_count, o_rows, levels, 128), f32),
            shape((128, 128), f32),
            shape((128, 128), f32),
            shape((2, q_count, levels, 128), f32),
            shape((2, levels, 128), f32),
            shape((4, o_rows, 128), i32),
        ],
        scratch_shapes=[
            V(weights.shape, bf16),
            V(inverses.shape, f32),
            V(ocean.shape, f32),
            V((q_count, o_rows, levels, 128), f32),
            V((mask.shape[0], 8, 128), f32),
            V((4 * pairs, 128), f32),
            V((2 * chips, 16, 128), f32),
            V((chips, 1, 128), f32),
            V((2 * chips, 16, 128), f32),
            V((chips, 1, 128), f32),
            V((2, 128, 128), f32),
            V((128, 128), f32),
            V((2, levels, 128), f32),
            V((128, 128), f32),
            V((2, 8, 128), f32),
            V((2, 8, 128), f32),
            V((2, 8, 128), f32),
            V((2, q_count, levels, 128), f32),
            V((2, levels, 128), f32),
            V((2, levels, 128), f32),
            V((2, 8, 128), f32),
            V((4, o_rows, 128), i32),
            V((2, 8, 128), f32),
            V((2, 8, 128), f32),
            DMA((11,)),
            DMA((4,)),
            DMA((12,)),
            DMA((12,)),
            DMA((5,)),
            DMA((5,)),
        ],
        compiler_params=pltpu.CompilerParams(
            collective_id=0, has_side_effects=True, vmem_limit_bytes=VMEM_BYTES
        ),
        name="couple",
    )(src, coupling, dest, block, atm, mask, depth, weights, inverses, ocean)


def finish_kernel(
    base_ref, force_ref, gain_ref, rows_ref, cols_ref, sides_ref, depth_ref, out_ref, mixed, keep
):
    q = pl.program_id(0)
    o_rows, levels = base_ref.shape[1:3]
    shape = (levels, 128)
    level = iota(shape, 0)
    cell = iota(shape, 1)

    @pl.when(q == 0)
    def _():
        def weigh(r, carry):
            count = jnp.zeros(shape, f32)
            for s in range(4):
                count = count + (level < sides_ref[s, pl.ds(r, 1), :]).astype(f32)
            keep[r] = 1.0 - diffusion_rate * count
            return carry

        lax.fori_loop(0, o_rows, weigh, 0)

    mixed[0] = rows_ref[0, 0]
    mixed[o_rows + 1] = rows_ref[1, 0]

    def pick(values, k):
        return jnp.take_along_axis(values, jnp.full(shape, k, i32), axis=1)

    def force(r, carry):
        k = q * o_rows + r
        gain = pick(gain_ref[pl.ds(0, levels), :], k)
        value = base_ref[0, r] + gain * force_ref[pl.ds(k, 1), :]
        mixed[r + 1] = jnp.where(level < depth_ref[pl.ds(r, 1), :], value, 0.0)
        return carry

    lax.fori_loop(0, o_rows, force, 0, unroll=2)

    def spread(r, carry):
        k = q * o_rows + r
        here = mixed[r + 1]
        west = jnp.where(cell == 0, pick(cols_ref[0], k), pltpu.roll(here, 1, 1))
        east = jnp.where(cell == 127, pick(cols_ref[1], k), pltpu.roll(here, 127, 1))
        around = (mixed[r] + mixed[r + 2]) + (west + east)
        value = keep[r] * here + diffusion_rate * around
        active = level < depth_ref[pl.ds(r, 1), :]
        out_ref[0, pl.ds(r, levels, stride=o_rows), :] = jnp.where(active, value, base_ref[0, r])
        return carry

    lax.fori_loop(0, o_rows, spread, 0, unroll=2)


def finish(base, force, gain, rows, cols, sides, depth):
    q_count, o_rows, levels, _ = base.shape
    full = lambda a: pl.BlockSpec(a.shape, lambda q: (0,) * a.ndim)
    return pl.pallas_call(
        finish_kernel,
        grid=(q_count,),
        in_specs=[
            pl.BlockSpec((1, o_rows, levels, 128), lambda q: (q, 0, 0, 0)),
            full(force),
            full(gain),
            pl.BlockSpec((2, 1, levels, 128), lambda q: (0, q, 0, 0)),
            full(cols),
            full(sides),
            full(depth),
        ],
        out_specs=pl.BlockSpec((1, levels * o_rows, 128), lambda q: (q, 0, 0)),
        out_shape=jax.ShapeDtypeStruct((q_count, levels * o_rows, 128), f32),
        scratch_shapes=[
            pltpu.VMEM((o_rows + 2, levels, 128), f32),
            pltpu.VMEM((o_rows, levels, 128), f32),
        ],
        compiler_params=pltpu.CompilerParams(vmem_limit_bytes=VMEM_BYTES),
        name="finish",
    )(base, force, gain, rows, cols, sides, depth)


def on_device(
    atm_flux,
    sea_mask,
    src_block,
    dest_dev,
    dest_block,
    intersection_weights,
    coupling,
    inverses,
    ocean_state,
    depth_levels,
):
    n_lat, n_lon = lax.axis_size("lat"), lax.axis_size("lon")
    pairs = src_block.shape[0]
    q_count, levels, o_rows, cells = ocean_state.shape
    base, force, gain, rows, cols, sides = couple(
        src_block, coupling, dest_dev.reshape(1, pairs), dest_block.reshape(1, pairs),
        atm_flux, sea_mask, depth_levels, intersection_weights,
        inverses.reshape(q_count, o_rows, levels, levels),
        ocean_state.reshape(q_count * levels * o_rows, cells), n_lat, n_lon,
    )
    out = finish(base, force, gain, rows, cols, sides, depth_levels)
    return out.reshape(ocean_state.shape)


def solution(mesh):
    placed = (
        P(None, "lat", "lon"),
        P("lat", "lon"),
        P(("lat", "lon")),
        P(("lat", "lon"), None),
        P(("lat", "lon")),
        P(("lat", "lon"), None, None),
        P(),
        P(None, "lat", "lon", None, None),
        P(None, None, "lat", "lon"),
        P("lat", "lon"),
    )
    return jax.shard_map(
        on_device,
        mesh=mesh,
        in_specs=placed,
        out_specs=P(None, None, "lat", "lon"),
        check_vma=False,
    )
```

time: 790 us -> 78 us (0.10)
  waiting for transfers between devices: 658 us -> 0 us
  Pallas kernels: 0 us -> 77.8 us
  other arithmetic: 46.5 us -> 0 us
  local copies, waits for them, and re-layouts: 37.8 us -> 0 us
  matrix products: 19.6 us -> 0 us
  between operations: 13.6 us -> 0.01 us
  starting transfers between devices: 13.1 us -> 0 us
    reduce_scatter x1 -> x0, waiting for transfers between devices: 652 us -> none  [on_device(): lax.psum_scatter(jnp.zeros((blocks_dev * lax.axis_size(('lat', 'lon')),)...]
    pallas_call x0 -> x2, Pallas kernels: none -> 77.8 us  [the longest x1 54.1 us: couple(): pl.pallas_call(functools.partial(couple_kernel, n_lat, n_lon), in_specs=[...]
    scatter-add x1 -> x0, other arithmetic: 25.2 us -> none  [on_device(): received = lax.psum_scatter(jnp.zeros((blocks_dev * lax.axis_size(('lat',...]
    dot_general x3 -> x0, matrix products: 19.6 us -> none  [the longest x1 13.7 us: on_device(): jnp.einsum('qrlm,qmrx->qlrx', inverses[:, :, 0], rhs, precision=lax.Preci...]
    add x1 -> x0, other arithmetic: 15.7 us -> none  [on_device(): mixed + diffusion_rate * jnp.where(active[None], total, jnp.float32(0.0))]
    slice x11 -> x0, local copies, waits for them, and re-layouts: 14.3 us -> none  [the longest x3 9.58 us: padded_2(): head = lax.slice_in_dim(cells, 0, width, axis=dim)]
    ppermute x8 -> x0, starting transfers between devices: 13.1 us -> none  [the longest x4 10.6 us: padded_2(): lax.ppermute(head, axis, [((i + 1) % count, i) for i in range(count)])]
  transfers between devices with their start and end apart: 9 -> 0, of which waited for: 4 -> 0; matrix products, arithmetic and copies ran while one was open for 2% -> 0% of each run, Pallas kernels for 0% -> 0%
where the time goes in v2:
time: 78 us; the launch traced here: 77.8 us
  Pallas kernels  77.8 us (100%)
    pallas_call x1, Pallas kernels, couple(): pl.pallas_call(functools.partial(couple_kernel, n_lat, n_lon), in_specs=[...  54.1 us
    pallas_call x1, Pallas kernels, finish(): pl.pallas_call(finish_kernel, grid=(q_count,), in_specs=[pl.BlockSpec((1,...  23.7 us

profile of v2, /device:TPU:0, one launch (start us, length us, event | category | flops | bytes accessed | tf_op | source)
XLA Modules:
  0.0 77.8 jit_solution(16835911254264208475)
XLA Ops:
  0.0 54.1 %couple.1 = (f32[4,32,80,128]{3,2,1,0:T(8,128)}, f32[128,128]{1,0:T(8,128)}, f32[128,128]{1,0:T(8,128)}, f32[2,4,80,128]{3,2,1,0:T(8,128)}, f32[2,80,128]{2,1,0:T(8,128)}, /*index=5*/s32[4,32,128]{2,1,0:T(8,128)}) custom-call(s32[256]{0:T(256)} %src_ref.1, f32[4,8]{1,0:T(4,128)} %coupling_ref.1, s32[1,256]{1,0:T(1,128)} %bitcast.7, s32[1,256]{1,0:T(1,128)} %bitcast.8, ...), custom_call_target="tpu_custom_call" | custom-call | tf_op jit(solution)/shard_map/couple/pallas_call | solution.py:331
  54.1 23.7 %finish.1 = f32[4,2560,128]{2,1,0:T(8,128)} custom-call(f32[4,32,80,128]{3,2,1,0:T(8,128)} %get-tuple-element.11.base_ref, f32[128,128]{1,0:T(8,128)} %get-tuple-element.12.force_ref, f32[128,128]{1,0:T(8,128)} %get-tuple-element.13.gain_ref, f32[2,4,80,128]{3,2,1,0:T(8,128)} %get-tuple-element.14.rows_ref, f32[2,80,128]{2,1,0:T(8,128)} %get-tuple-element.15.cols_ref, ...), custom_call_target="tpu_custom_call" | custom-call | tf_op jit(solution)/shard_map/finish/pallas_call | solution.py:434

commit v3 on v2

--- a/solution.py
+++ b/solution.py
@@ -11,6 +11,7 @@
 CAP = 4
 MESH = pl.DeviceIdType.MESH
 NORTH, SOUTH, WEST, EAST = range(4)
+ORDER = (2, 1, 3, 0)
 f32, bf16, i32 = jnp.float32, jnp.bfloat16, jnp.int32
 VMEM_BYTES = 62 << 20
 
@@ -37,9 +38,9 @@
     src_ref, coupling_ref, dest_ref, block_ref, atm_ref, mask_ref, depth_ref,
     weights_hbm, inverses_hbm, ocean_hbm,
     base_hbm, force_ref, gain_ref, rows_ref, cols_ref, sides_ref,
-    weights, inverses, ocean, base, table, contrib,
+    weights, inverses, ocean, skewed, table, contrib,
     send, meta, recv, recv_meta, partial, partial_in,
-    col_out, gain_t, gain_out, force_out, strip_out,
+    packed, col_out, gain_out, force_out, strip_out, row_out,
     row_in, col_in, gain_in, gain_strip_in, depth_in, force_in, strip_in,
     load_sems, ship_sems, halo_send, halo_recv, force_send, force_recv,
 ):
@@ -51,6 +52,7 @@
     q_count = coupling_ref.shape[0]
     pairs = dest_ref.shape[1]
     levels = inverses.shape[2]
+    skew = skewed.shape[0] // levels
     o_rows = depth_ref.shape[0]
 
     w_chunks = 8
@@ -69,11 +71,24 @@
 
     barrier = pltpu.get_barrier_semaphore()
 
-    def peer(k):
-        x = (lon // 8 + k) % 4
-        y = (lon // 2 + k // 4) % 4
-        z = (lat + k // 16) % 4
-        return z, (x * 4 + y) * 2 + core
+    x_here, y_here = lon // 8, lon // 2 % 4
+
+    def plane(dz, each, first=0):
+        z = lax.rem(lat + dz, n_lat)
+        xs = [lax.rem(x_here + dx, 4) * 8 + core for dx in range(4)]
+
+        def line(dy, carry):
+            y = lax.rem(y_here + dy, 4) * 2
+            for dx in range(4):
+                each(z, xs[dx] + y)
+            return carry
+
+        if dz == 0:
+            for dx in range(1, 4):
+                each(z, xs[dx] + y_here * 2)
+            lax.fori_loop(1, 4, line, 0)
+        else:
+            lax.fori_loop(0, 4, line, 0)
 
     beside = {
         NORTH: ((lat + n_lat - 1) % n_lat, lon),
@@ -83,11 +98,11 @@
     }
     partner = (lat, lon + 1 - 2 * core)
 
-    def greet(k, carry):
-        pl.semaphore_signal(barrier, inc=1, device_id=peer(k), device_id_type=MESH)
-        return carry
-
-    lax.fori_loop(1, chips, greet, 0)
+    def greet(z, o):
+        pl.semaphore_signal(barrier, inc=1, device_id=(z, o), device_id_type=MESH)
+
+    for dz in range(n_lat):
+        plane(dz, greet)
     for side in (WEST, EAST):
         pl.semaphore_signal(barrier, inc=1, device_id=beside[side], device_id_type=MESH)
 
@@ -150,71 +165,95 @@
             [contrib[pl.ds(h * 2 * pairs, 2 * pairs), :] for h in range(2)], axis=1
         )
     )
-    chunk = 256
-
-    def place(i, carry):
+    chunk = devices * 8 // n_lat
+    send_sem, meta_send_sem = ship_sems.at[0], ship_sems.at[1]
+    recv_sems = [ship_sems.at[2 + dz] for dz in range(n_lat)]
+    meta_recv_sems = [ship_sems.at[2 + n_lat + dz] for dz in range(n_lat)]
+
+    def place(i):
         hot = one_hot(iota((chunk, 2 * pairs), 0) + i * chunk == keys)
         out = dot(hot, high) + dot(hot, low)
         for h in range(2):
             send[pl.ds(i * (chunk // 8), chunk // 8), pl.ds(h * 8, 8), :] = out[
                 :, h * 128 : (h + 1) * 128
             ].reshape(chunk // 8, 8, 128)
-        return carry
-
-    lax.fori_loop(0, devices * 8 // chunk, place, 0)
-
-    pl.semaphore_wait(barrier, chips + 1)
-    send_sem, recv_sem, meta_send_sem, meta_recv_sem = (ship_sems.at[i] for i in range(4))
-
-    def ship(k, carry):
-        z, o = peer(k)
-        to = z * (n_lon // 2) + o // 2
-        pltpu.make_async_remote_copy(
-            send.at[pl.ds(2 * to, 2)], recv.at[pl.ds(2 * my_chip, 2)], send_sem, recv_sem,
-            device_id=(z, o), device_id_type=MESH,
-        ).start()
-        pltpu.make_async_remote_copy(
-            meta.at[to], recv_meta.at[my_chip], meta_send_sem, meta_recv_sem,
-            device_id=(z, o), device_id_type=MESH,
-        ).start()
-        return carry
-
-    lax.fori_loop(1, chips, ship, 0)
+
     mine = pl.ds(2 * my_chip, 2)
-    pltpu.make_async_copy(send.at[mine], recv.at[mine], recv_sem).start()
-    pltpu.make_async_copy(meta.at[my_chip], recv_meta.at[my_chip], meta_recv_sem).start()
+    for n, dz in enumerate(ORDER):
+        place(lax.rem(lat + dz, n_lat))
+        if n == 0:
+            pl.semaphore_wait(barrier, chips + 1)
+
+        def ship(z, o):
+            to = z * (n_lon // 2) + o // 2
+            pltpu.make_async_remote_copy(
+                send.at[pl.ds(2 * to, 2)], recv.at[mine], send_sem, recv_sems[dz],
+                device_id=(z, o), device_id_type=MESH,
+            ).start()
+            pltpu.make_async_remote_copy(
+                meta.at[to], recv_meta.at[my_chip], meta_send_sem, meta_recv_sems[dz],
+                device_id=(z, o), device_id_type=MESH,
+            ).start()
+
+        plane(dz, ship)
+    pltpu.make_async_copy(send.at[mine], recv.at[mine], recv_sems[0]).start()
+    pltpu.make_async_copy(meta.at[my_chip], recv_meta.at[my_chip], meta_recv_sems[0]).start()
 
     inverse_copy.wait()
     ocean_copy.wait()
-    gain_ref[...] = jnp.zeros_like(gain_ref)
+    packed[...] = jnp.zeros_like(packed)
     level = iota((levels, 128), 0)
     lane_id = iota((levels, 128), 1)
-
-    def mix(i, carry):
-        q, r = i // o_rows, i % o_rows
-        state = ocean[pl.ds(q * levels * o_rows + r, levels, stride=o_rows), :]
-        active = level < depth_ref[pl.ds(r, 1), :]
-        inverse = inverses[q, r]
-        left = jnp.concatenate(halves(inverse), axis=0)
-        right = jnp.concatenate(halves(jnp.where(active, state, 0.0)), axis=1)
-        out = dot(left, right)
-        solved = out[:levels, :128] + (out[:levels, 128:] + out[levels:, :128])
-        mixed = jnp.where(active, solved, state)
-        base[q, r] = mixed
-        here = lane_id == i
-        col_out[0] = jnp.where(here, jnp.broadcast_to(mixed[:, :1], mixed.shape), col_out[0])
-        col_out[1] = jnp.where(here, jnp.broadcast_to(mixed[:, 127:], mixed.shape), col_out[1])
-        gain_ref[pl.ds(0, levels), :] = jnp.where(
-            here, jnp.broadcast_to(inverse[:, :1], mixed.shape), gain_ref[pl.ds(0, levels), :]
-        )
+    low_levels = pl.ds(0, levels)
+
+    def copy_out(q):
+        return pltpu.make_async_copy(ocean.at[q], base_hbm.at[q], load_sems.at[w_chunks + 2 + q])
+
+    def field(q, carry):
+        def skew_in(l, carry):
+            skewed[pl.ds(l * skew, o_rows), :] = ocean[q, l]
+            return carry
+
+        lax.fori_loop(0, levels, skew_in, 0, unroll=8)
+
+        def mix(r, carry):
+            i = q * o_rows + r
+            column = pl.ds(r, levels, stride=skew)
+            state = skewed[column, :]
+            active = level < depth_ref[pl.ds(r, 1), :]
+            inverse = inverses[q, r]
+            left = jnp.concatenate(halves(inverse), axis=0)
+            right = jnp.concatenate(halves(jnp.where(active, state, 0.0)), axis=1)
+            out = dot(left, right)
+            solved = out[:levels, :128] + (out[:levels, 128:] + out[levels:, :128])
+            mixed = jnp.where(active, solved, state)
+            skewed[column, :] = mixed
+            turned = pltpu.roll(mixed, i, 1)
+            packed[0, low_levels, :] = jnp.where(lane_id == i, turned, packed[0, low_levels, :])
+            last = lax.rem(i + 127, 128)
+            packed[1, low_levels, :] = jnp.where(lane_id == last, turned, packed[1, low_levels, :])
+            gain = jnp.broadcast_to(inverse[:, :1], mixed.shape)
+            packed[2, low_levels, :] = jnp.where(lane_id == i, gain, packed[2, low_levels, :])
+            return carry
+
+        lax.fori_loop(0, o_rows, mix, 0, unroll=2)
+
+        def skew_out(l, carry):
+            ocean[q, l] = skewed[pl.ds(l * skew, o_rows), :]
+            return carry
+
+        lax.fori_loop(0, levels, skew_out, 0, unroll=8)
+        for s, r in ((0, 0), (1, o_rows - 1)):
+            row_out[s, q] = skewed[pl.ds(r, levels, stride=skew), :]
+        copy_out(q).start()
         return carry
 
-    lax.fori_loop(0, q_count * o_rows, mix, 0, unroll=2)
-    base_copy = pltpu.make_async_copy(base, base_hbm, load_sems.at[w_chunks + 2])
-    base_copy.start()
-    gain_t[...] = jnp.transpose(gain_ref[...])
+    lax.fori_loop(0, q_count, field, 0)
+    col_out[0] = jnp.transpose(packed[0])
+    col_out[1] = jnp.transpose(pltpu.roll(packed[1], 1, 1))
+    gain_ref[...] = jnp.transpose(packed[2])
     for s, r in ((0, 0), (1, o_rows - 1)):
-        gain_out[s, pl.ds(0, q_count), :] = gain_t[pl.ds(r, q_count, stride=o_rows), :]
+        gain_out[s, pl.ds(0, q_count), :] = gain_ref[pl.ds(r, q_count, stride=o_rows), :]
 
     copies = []
 
@@ -228,33 +267,36 @@
         copy.start()
         copies.append(copy)
 
-    for side, r in ((NORTH, 0), (SOUTH, o_rows - 1)):
-        hand(side, base.at[:, r], lambda o: row_in.at[o])
+    for side in (NORTH, SOUTH):
+        hand(side, row_out.at[side], lambda o: row_in.at[o])
         hand(side, gain_out.at[side], lambda o: gain_strip_in.at[o])
     for side in (WEST, EAST):
         hand(side, col_out.at[side - 2], lambda o: col_in.at[o - 2])
-        hand(side, gain_ref.at[pl.ds(0, levels)], lambda o: gain_in.at[o - 2])
+        hand(side, gain_ref, lambda o: gain_in.at[o - 2])
     for side in range(4):
         hand(side, depth_ref, lambda o: depth_in.at[o])
     for copy in copies:
         copy.wait()
 
-    every = pl.ds(0, chips)
-    pltpu.make_async_copy(recv_meta, recv_meta, meta_recv_sem).wait()
-    pltpu.make_async_copy(recv, recv, recv_sem).wait()
     partial[...] = jnp.zeros_like(partial)
-
-    def add(i, carry):
-        at = i * 8
-        keys = jnp.concatenate(
-            [jnp.sum(recv_meta[pl.ds(at + 4 * h, 4)], axis=0) for h in range(2)], axis=1
-        ).astype(i32)
-        hot = one_hot(iota((256, 256), 0) == keys)
-        high, low = halves(recv[pl.ds(2 * at, 16)].reshape(256, 128))
-        partial[...] += (dot(hot, high) + dot(hot, low)).reshape(2, 128, 128)
-        return carry
-
-    lax.fori_loop(0, chips // 8, add, 0)
+    per_plane = chips // n_lat
+    for dz in ORDER:
+        z = lax.rem(lat + n_lat - dz, n_lat)
+        some = pl.ds(z * per_plane, per_plane)
+        pltpu.make_async_copy(recv_meta.at[some], recv_meta.at[some], meta_recv_sems[dz]).wait()
+        some = pl.ds(z * 2 * per_plane, 2 * per_plane)
+        pltpu.make_async_copy(recv.at[some], recv.at[some], recv_sems[dz]).wait()
+        out = None
+        for i in range(per_plane // 8):
+            at = z * per_plane + i * 8
+            keys = jnp.concatenate(
+                [jnp.sum(recv_meta[pl.ds(at + 4 * h, 4)], axis=0) for h in range(2)], axis=1
+            ).astype(i32)
+            hot = one_hot(iota((256, 256), 0) == keys)
+            both = jnp.concatenate(halves(recv[pl.ds(2 * at, 16)].reshape(256, 128)), axis=1)
+            out = dot(hot, both) if out is None else out + dot(hot, both)
+        partial[...] += (out[:, :128] + out[:, 128:]).reshape(2, 128, 128)
+
     swap = pltpu.make_async_remote_copy(
         partial.at[1 - core], partial_in, force_send.at[4], force_recv.at[4],
         device_id=partner, device_id_type=MESH,
@@ -291,11 +333,10 @@
     )
     sides_ref[WEST] = jnp.where(cell_id == 0, roll(depth_in[WEST], 1, 1), roll(depth, 1, 1))
     sides_ref[EAST] = jnp.where(cell_id == 127, roll(depth_in[EAST], 127, 1), roll(depth, 127, 1))
-    turned = [
-        jnp.transpose(jnp.concatenate([depth_in[s].astype(f32)] * q_count, axis=0))
-        for s in (WEST, EAST)
+    limits = [
+        jnp.concatenate([jnp.broadcast_to(edge, (o_rows, 128))] * q_count, axis=0)
+        for edge in (depth_in[WEST][:, 127:], depth_in[EAST][:, :1])
     ]
-    limits = turned[0][127:].astype(i32), turned[1][:1].astype(i32)
     strips = jnp.transpose(
         jnp.concatenate(
             [gain_strip_in[0], gain_strip_in[1], jnp.zeros((112, 128), f32)], axis=0
@@ -309,14 +350,21 @@
             gain = jnp.broadcast_to(strips[:levels, s * 8 + q : s * 8 + q + 1], (levels, 128))
             value = row_in[s, q] + gain * force_in[s, pl.ds(q, 1), :]
             rows_ref[s, q] = jnp.where(level < edges[s], value, 0.0)
-        value = col_in[s] + gain_in[s] * strip_in[s, pl.ds(0, 1), :]
-        cols_ref[s] = jnp.where(level < limits[s], value, 0.0)
+    level_lane = iota((128, 128), 1)
+    edge = []
+    for s in range(2):
+        strip = jnp.transpose(jnp.broadcast_to(strip_in[s, pl.ds(0, 1), :], (128, 128)))
+        value = col_in[s] + gain_in[s] * strip
+        edge.append(jnp.where(level_lane < limits[s], value, 0.0))
+    cols_ref[0] = jnp.where(level_lane < 64, edge[0], roll(edge[1], 64, 1))
+    cols_ref[1] = jnp.where(level_lane < 64, roll(edge[0], 64, 1), edge[1])
 
     rest = pl.ds(0, 2 * (chips - 1))
     pltpu.make_async_copy(send.at[rest], send.at[rest], send_sem).wait()
     rest = pl.ds(0, chips - 1)
     pltpu.make_async_copy(meta.at[rest], meta.at[rest], meta_send_sem).wait()
-    base_copy.wait()
+    for q in range(q_count):
+        copy_out(q).wait()
 
 
 def couple(src, coupling, dest, block, atm, mask, depth, weights, inverses, ocean, n_lat, n_lon):
@@ -333,18 +381,18 @@
         in_specs=[smem, smem] + [vmem] * 5 + [hbm] * 3,
         out_specs=[hbm] + [vmem] * 5,
         out_shape=[
-            shape((q_count, o_rows, levels, 128), f32),
+            shape((q_count, levels, o_rows, 128), f32),
             shape((128, 128), f32),
             shape((128, 128), f32),
             shape((2, q_count, levels, 128), f32),
-            shape((2, levels, 128), f32),
+            shape((2, 128, 128), f32),
             shape((4, o_rows, 128), i32),
         ],
         scratch_shapes=[
             V(weights.shape, bf16),
             V(inverses.shape, f32),
             V(ocean.shape, f32),
-            V((q_count, o_rows, levels, 128), f32),
+            V((levels * (o_rows + 1), 128), f32),
             V((mask.shape[0], 8, 128), f32),
             V((4 * pairs, 128), f32),
             V((2 * chips, 16, 128), f32),
@@ -353,20 +401,21 @@
             V((chips, 1, 128), f32),
             V((2, 128, 128), f32),
             V((128, 128), f32),
-            V((2, levels, 128), f32),
-            V((128, 128), f32),
+            V((3, 128, 128), f32),
+            V((2, 128, 128), f32),
             V((2, 8, 128), f32),
             V((2, 8, 128), f32),
             V((2, 8, 128), f32),
             V((2, q_count, levels, 128), f32),
-            V((2, levels, 128), f32),
-            V((2, levels, 128), f32),
+            V((2, q_count, levels, 128), f32),
+            V((2, 128, 128), f32),
+            V((2, 128, 128), f32),
             V((2, 8, 128), f32),
             V((4, o_rows, 128), i32),
             V((2, 8, 128), f32),
             V((2, 8, 128), f32),
-            DMA((11,)),
-            DMA((4,)),
+            DMA((14,)),
+            DMA((10,)),
             DMA((12,)),
             DMA((12,)),
             DMA((5,)),
@@ -380,74 +429,86 @@
 
 
 def finish_kernel(
-    base_ref, force_ref, gain_ref, rows_ref, cols_ref, sides_ref, depth_ref, out_ref, mixed, keep
+    base_ref, force_ref, gain_ref, rows_ref, cols_ref, sides_ref, depth_ref, out_ref, slab, keep
 ):
-    q = pl.program_id(0)
-    o_rows, levels = base_ref.shape[1:3]
-    shape = (levels, 128)
-    level = iota(shape, 0)
+    q, part = pl.program_id(0), pl.program_id(1)
+    levels, o_rows = base_ref.shape[1:3]
+    shape = (o_rows, 128)
     cell = iota(shape, 1)
+    first = part * levels
 
     @pl.when(q == 0)
     def _():
-        def weigh(r, carry):
+        def weigh(l, carry):
             count = jnp.zeros(shape, f32)
             for s in range(4):
-                count = count + (level < sides_ref[s, pl.ds(r, 1), :]).astype(f32)
-            keep[r] = 1.0 - diffusion_rate * count
+                count = count + jnp.where(first + l < sides_ref[s], diffusion_rate, 0.0)
+            keep[first + l] = 1.0 - count
             return carry
 
-        lax.fori_loop(0, o_rows, weigh, 0)
-
-    mixed[0] = rows_ref[0, 0]
-    mixed[o_rows + 1] = rows_ref[1, 0]
-
-    def pick(values, k):
-        return jnp.take_along_axis(values, jnp.full(shape, k, i32), axis=1)
-
-    def force(r, carry):
-        k = q * o_rows + r
-        gain = pick(gain_ref[pl.ds(0, levels), :], k)
-        value = base_ref[0, r] + gain * force_ref[pl.ds(k, 1), :]
-        mixed[r + 1] = jnp.where(level < depth_ref[pl.ds(r, 1), :], value, 0.0)
+        lax.fori_loop(0, levels, weigh, 0, unroll=4)
+
+    here = pl.ds(q * o_rows, o_rows)
+    together = slab.shape[0] // 2
+    groups = levels // together
+
+    def force(group):
+        at = lax.rem(group, 2) * together
+        for j in range(together):
+            i = group * together + j
+            l = first + i
+            gain = jnp.take_along_axis(gain_ref[here, :], jnp.full(shape, l, i32), axis=1)
+            mixed = base_ref[0, i] + gain * force_ref[here, :]
+            slab[at + j, pl.ds(8, o_rows), :] = jnp.where(l < depth_ref[...], mixed, 0.0)
+            slab[at + j, pl.ds(7, 1), :] = rows_ref[0, 0, pl.ds(i, 1), :]
+            slab[at + j, pl.ds(8 + o_rows, 1), :] = rows_ref[1, 0, pl.ds(i, 1), :]
+
+    def spread(group):
+        at = lax.rem(group, 2) * together
+        for j in range(together):
+            i = group * together + j
+            l = first + i
+            spot = l % 64 + jnp.where(cell == 127, 64, 0)
+            edge = jnp.take_along_axis(cols_ref[l // 64, here, :], spot, axis=1)
+            mixed = slab[at + j, pl.ds(8, o_rows), :]
+            west = jnp.where(cell == 0, edge, pltpu.roll(mixed, 1, 1))
+            east = jnp.where(cell == 127, edge, pltpu.roll(mixed, 127, 1))
+            beside = slab[at + j, pl.ds(7, o_rows), :] + slab[at + j, pl.ds(9, o_rows), :]
+            value = keep[l] * mixed + diffusion_rate * (beside + (west + east))
+            out_ref[0, i] = jnp.where(l < depth_ref[...], value, base_ref[0, i])
+
+    force(0)
+
+    def step(group, carry):
+        spread(group)
+        force(lax.rem(group + 1, groups))
         return carry
 
-    lax.fori_loop(0, o_rows, force, 0, unroll=2)
-
-    def spread(r, carry):
-        k = q * o_rows + r
-        here = mixed[r + 1]
-        west = jnp.where(cell == 0, pick(cols_ref[0], k), pltpu.roll(here, 1, 1))
-        east = jnp.where(cell == 127, pick(cols_ref[1], k), pltpu.roll(here, 127, 1))
-        around = (mixed[r] + mixed[r + 2]) + (west + east)
-        value = keep[r] * here + diffusion_rate * around
-        active = level < depth_ref[pl.ds(r, 1), :]
-        out_ref[0, pl.ds(r, levels, stride=o_rows), :] = jnp.where(active, value, base_ref[0, r])
-        return carry
-
-    lax.fori_loop(0, o_rows, spread, 0, unroll=2)
+    lax.fori_loop(0, groups, step, 0)
 
 
 def finish(base, force, gain, rows, cols, sides, depth):
-    q_count, o_rows, levels, _ = base.shape
-    full = lambda a: pl.BlockSpec(a.shape, lambda q: (0,) * a.ndim)
+    q_count, levels, o_rows, _ = base.shape
+    parts = 2
+    full = lambda a: pl.BlockSpec(a.shape, lambda q, p: (0,) * a.ndim)
+    block = pl.BlockSpec((1, levels // parts, o_rows, 128), lambda q, p: (q, p, 0, 0))
     return pl.pallas_call(
         finish_kernel,
-        grid=(q_count,),
+        grid=(q_count, parts),
         in_specs=[
-            pl.BlockSpec((1, o_rows, levels, 128), lambda q: (q, 0, 0, 0)),
+            block,
             full(force),
             full(gain),
-            pl.BlockSpec((2, 1, levels, 128), lambda q: (0, q, 0, 0)),
+            pl.BlockSpec((2, 1, levels // parts, 128), lambda q, p: (0, q, p, 0)),
             full(cols),
             full(sides),
             full(depth),
         ],
-        out_specs=pl.BlockSpec((1, levels * o_rows, 128), lambda q: (q, 0, 0)),
-        out_shape=jax.ShapeDtypeStruct((q_count, levels * o_rows, 128), f32),
+        out_specs=block,
+        out_shape=jax.ShapeDtypeStruct(base.shape, f32),
         scratch_shapes=[
-            pltpu.VMEM((o_rows + 2, levels, 128), f32),
-            pltpu.VMEM((o_rows, levels, 128), f32),
+            pltpu.VMEM((8, o_rows + 16, 128), f32),
+            pltpu.VMEM((levels, o_rows, 128), f32),
         ],
         compiler_params=pltpu.CompilerParams(vmem_limit_bytes=VMEM_BYTES),
         name="finish",
@@ -473,10 +534,9 @@
         src_block, coupling, dest_dev.reshape(1, pairs), dest_block.reshape(1, pairs),
         atm_flux, sea_mask, depth_levels, intersection_weights,
         inverses.reshape(q_count, o_rows, levels, levels),
-        ocean_state.reshape(q_count * levels * o_rows, cells), n_lat, n_lon,
-    )
-    out = finish(base, force, gain, rows, cols, sides, depth_levels)
-    return out.reshape(ocean_state.shape)
+        ocean_state, n_lat, n_lon,
+    )
+    return finish(base, force, gain, rows, cols, sides, depth_levels)
 
 
 def solution(mesh):

time: 78 us -> 63.4 us (0.81)
  Pallas kernels: 77.8 us -> 63.2 us
    pallas_call x1, Pallas kernels: 54.1 us -> 46.2 us  [couple(): pl.pallas_call(functools.partial(couple_kernel, n_lat, n_lon), in_specs=[...]
    pallas_call x1, Pallas kernels: 23.7 us -> 17.1 us  [finish(): pl.pallas_call(finish_kernel, grid=(q_count, parts), in_specs=[block, ful...]
where the time goes in v3:
time: 63.4 us; the launch traced here: 63.2 us
  Pallas kernels  63.2 us (100%)
    pallas_call x1, Pallas kernels, couple(): pl.pallas_call(functools.partial(couple_kernel, n_lat, n_lon), in_specs=[...  46.2 us
    pallas_call x1, Pallas kernels, finish(): pl.pallas_call(finish_kernel, grid=(q_count, parts), in_specs=[block, ful...  17.1 us

profile of v3, /device:TPU:0, one launch (start us, length us, event | category | flops | bytes accessed | tf_op | source)
XLA Modules:
  0.0 63.2 jit_solution(17648482514214510527)
XLA Ops:
  0.0 46.2 %couple.1 = (f32[4,80,32,128]{3,2,1,0:T(8,128)}, f32[128,128]{1,0:T(8,128)}, f32[128,128]{1,0:T(8,128)}, f32[2,4,80,128]{3,2,1,0:T(8,128)}, f32[2,128,128]{2,1,0:T(8,128)}, /*index=5*/s32[4,32,128]{2,1,0:T(8,128)}) custom-call(s32[256]{0:T(256)} %src_ref.1, f32[4,8]{1,0:T(4,128)} %coupling_ref.1, s32[1,256]{1,0:T(1,128)} %bitcast.4, s32[1,256]{1,0:T(1,128)} %bitcast.5, ...), custom_call_target="tpu_custom_call" | custom-call | tf_op jit(solution)/shard_map/couple/pallas_call | solution.py:379
  46.2 17.1 %finish.1 = f32[4,80,32,128]{3,2,1,0:T(8,128)} custom-call(f32[4,80,32,128]{3,2,1,0:T(8,128)} %get-tuple-element.11.base_ref, f32[128,128]{1,0:T(8,128)} %get-tuple-element.12.force_ref, f32[128,128]{1,0:T(8,128)} %get-tuple-element.13.gain_ref, f32[2,4,80,128]{3,2,1,0:T(8,128)} %get-tuple-element.14.rows_ref, f32[2,128,128]{2,1,0:T(8,128)} %get-tuple-element.15.cols_ref, ...), custom_call_target="tpu_custom_call" | custom-call | tf_op jit(solution)/shard_map/finish/pallas_call | solution.py:495

commit v4 on v3

--- a/solution.py
+++ b/solution.py
@@ -42,7 +42,7 @@
     send, meta, recv, recv_meta, partial, partial_in,
     packed, col_out, gain_out, force_out, strip_out, row_out,
     row_in, col_in, gain_in, gain_strip_in, depth_in, force_in, strip_in,
-    load_sems, ship_sems, halo_send, halo_recv, force_send, force_recv,
+    load_sems, ship_sems, row_sems, halo_send, halo_recv, force_send, force_recv,
 ):
     chips = n_lat * n_lon // 2
     devices = 2 * chips
@@ -208,6 +208,13 @@
 
     def copy_out(q):
         return pltpu.make_async_copy(ocean.at[q], base_hbm.at[q], load_sems.at[w_chunks + 2 + q])
+
+    def row_copy(side, q):
+        return pltpu.make_async_remote_copy(
+            row_out.at[side, q], row_in.at[1 - side, q],
+            row_sems.at[side, q], row_sems.at[3 - side, q],
+            device_id=beside[side], device_id_type=MESH,
+        )
 
     def field(q, carry):
         def skew_in(l, carry):
@@ -236,7 +243,7 @@
             packed[2, low_levels, :] = jnp.where(lane_id == i, gain, packed[2, low_levels, :])
             return carry
 
-        lax.fori_loop(0, o_rows, mix, 0, unroll=2)
+        lax.fori_loop(0, o_rows, mix, 0, unroll=4)
 
         def skew_out(l, carry):
             ocean[q, l] = skewed[pl.ds(l * skew, o_rows), :]
@@ -246,6 +253,8 @@
         for s, r in ((0, 0), (1, o_rows - 1)):
             row_out[s, q] = skewed[pl.ds(r, levels, stride=skew), :]
         copy_out(q).start()
+        for side in (NORTH, SOUTH):
+            row_copy(side, q).start()
         return carry
 
     lax.fori_loop(0, q_count, field, 0)
@@ -267,16 +276,13 @@
         copy.start()
         copies.append(copy)
 
+    for side in range(4):
+        hand(side, depth_ref, lambda o: depth_in.at[o])
     for side in (NORTH, SOUTH):
-        hand(side, row_out.at[side], lambda o: row_in.at[o])
         hand(side, gain_out.at[side], lambda o: gain_strip_in.at[o])
     for side in (WEST, EAST):
         hand(side, col_out.at[side - 2], lambda o: col_in.at[o - 2])
         hand(side, gain_ref, lambda o: gain_in.at[o - 2])
-    for side in range(4):
-        hand(side, depth_ref, lambda o: depth_in.at[o])
-    for copy in copies:
-        copy.wait()
 
     partial[...] = jnp.zeros_like(partial)
     per_plane = chips // n_lat
@@ -321,6 +327,11 @@
         copy.start()
         forces.append(copy)
 
+    for copy in copies:
+        copy.wait()
+    for q in range(q_count):
+        for side in (NORTH, SOUTH):
+            row_copy(side, q).wait()
     depth = depth_ref[...]
     in_band = (lat > 0).astype(i32), (lat < n_lat - 1).astype(i32)
     north_depth = depth_in[NORTH] * in_band[0]
@@ -416,6 +427,7 @@
             V((2, 8, 128), f32),
             DMA((14,)),
             DMA((10,)),
+            DMA((4, q_count)),
             DMA((12,)),
             DMA((12,)),
             DMA((5,)),
@@ -429,77 +441,78 @@
 
 
 def finish_kernel(
-    base_ref, force_ref, gain_ref, rows_ref, cols_ref, sides_ref, depth_ref, out_ref, slab, keep
+    base_ref, force_ref, gain_ref, rows_ref, cols_ref, sides_ref, depth_ref, out_ref,
+    slabs, splits, sums, keep,
 ):
-    q, part = pl.program_id(0), pl.program_id(1)
+    q = pl.program_id(0)
     levels, o_rows = base_ref.shape[1:3]
     shape = (o_rows, 128)
     cell = iota(shape, 1)
-    first = part * levels
+    here = pl.ds(q * o_rows, o_rows)
+    group = slabs[0].shape[0]
+    groups = levels // group
+    first, last = cell == 0, cell == 127
+    rim = first | last
+    far = jnp.where(last, 64, 0)
+    apart = iota((256, 128), 0) % 128 - iota((256, 128), 1)
+    beside = one_hot((apart == 1) | (apart == -1))
 
     @pl.when(q == 0)
     def _():
         def weigh(l, carry):
             count = jnp.zeros(shape, f32)
             for s in range(4):
-                count = count + jnp.where(first + l < sides_ref[s], diffusion_rate, 0.0)
-            keep[first + l] = 1.0 - count
+                count = count + jnp.where(l < sides_ref[s], diffusion_rate, 0.0)
+            keep[l] = 1.0 - count
             return carry
 
         lax.fori_loop(0, levels, weigh, 0, unroll=4)
 
-    here = pl.ds(q * o_rows, o_rows)
-    together = slab.shape[0] // 2
-    groups = levels // together
-
-    def force(group):
-        at = lax.rem(group, 2) * together
-        for j in range(together):
-            i = group * together + j
-            l = first + i
-            gain = jnp.take_along_axis(gain_ref[here, :], jnp.full(shape, l, i32), axis=1)
-            mixed = base_ref[0, i] + gain * force_ref[here, :]
-            slab[at + j, pl.ds(8, o_rows), :] = jnp.where(l < depth_ref[...], mixed, 0.0)
-            slab[at + j, pl.ds(7, 1), :] = rows_ref[0, 0, pl.ds(i, 1), :]
-            slab[at + j, pl.ds(8 + o_rows, 1), :] = rows_ref[1, 0, pl.ds(i, 1), :]
-
-    def spread(group):
-        at = lax.rem(group, 2) * together
-        for j in range(together):
-            i = group * together + j
-            l = first + i
-            spot = l % 64 + jnp.where(cell == 127, 64, 0)
-            edge = jnp.take_along_axis(cols_ref[l // 64, here, :], spot, axis=1)
-            mixed = slab[at + j, pl.ds(8, o_rows), :]
-            west = jnp.where(cell == 0, edge, pltpu.roll(mixed, 1, 1))
-            east = jnp.where(cell == 127, edge, pltpu.roll(mixed, 127, 1))
-            beside = slab[at + j, pl.ds(7, o_rows), :] + slab[at + j, pl.ds(9, o_rows), :]
-            value = keep[l] * mixed + diffusion_rate * (beside + (west + east))
-            out_ref[0, i] = jnp.where(l < depth_ref[...], value, base_ref[0, i])
-
-    force(0)
-
-    def step(group, carry):
-        spread(group)
-        force(lax.rem(group + 1, groups))
-        return carry
-
-    lax.fori_loop(0, groups, step, 0)
+    def force(n, j):
+        slab, split, l = slabs[n % 2], splits[n % 2], n * group + j
+        gain = jnp.take_along_axis(gain_ref[here, :], jnp.full(shape, l, i32), axis=1)
+        mixed = base_ref[0, l] + gain * force_ref[here, :]
+        mixed = jnp.where(l < depth_ref[...], mixed, 0.0)
+        slab[j, pl.ds(8, o_rows), :] = mixed
+        slab[j, pl.ds(7, 1), :] = rows_ref[0, 0, pl.ds(l, 1), :]
+        slab[j, pl.ds(8 + o_rows, 1), :] = rows_ref[1, 0, pl.ds(l, 1), :]
+        high, low = halves(mixed)
+        split[pl.ds(j * o_rows, o_rows), pl.ds(0, 128)] = high
+        split[pl.ds(j * o_rows, o_rows), pl.ds(128, 128)] = low
+
+    def spread(n, j):
+        slab, total, l = slabs[n % 2], sums[n % 2], n * group + j
+        edge = jnp.take_along_axis(cols_ref[l // 64, here, :], far + l % 64, axis=1)
+        near = slab[j, pl.ds(7, o_rows), :] + slab[j, pl.ds(9, o_rows), :]
+        near = near + total[pl.ds(j * o_rows, o_rows), :]
+        near = near + jnp.where(rim, edge, 0.0)
+        value = keep[l] * slab[j, pl.ds(8, o_rows), :] + diffusion_rate * near
+        out_ref[0, l] = jnp.where(l < depth_ref[...], value, base_ref[0, l])
+
+    for j in range(group):
+        force(0, j)
+    for n in range(groups):
+        sums[n % 2][...] = dot(splits[n % 2][...], beside)
+        for j in range(group):
+            if n + 1 < groups:
+                force(n + 1, j)
+            spread(n, j)
 
 
 def finish(base, force, gain, rows, cols, sides, depth):
     q_count, levels, o_rows, _ = base.shape
-    parts = 2
-    full = lambda a: pl.BlockSpec(a.shape, lambda q, p: (0,) * a.ndim)
-    block = pl.BlockSpec((1, levels // parts, o_rows, 128), lambda q, p: (q, p, 0, 0))
+    group = 16
+    full = lambda a: pl.BlockSpec(a.shape, lambda q: (0,) * a.ndim)
+    block = pl.BlockSpec((1, levels, o_rows, 128), lambda q: (q, 0, 0, 0))
+    V = pltpu.VMEM
     return pl.pallas_call(
         finish_kernel,
-        grid=(q_count, parts),
+        grid=(q_count,),
         in_specs=[
             block,
             full(force),
             full(gain),
-            pl.BlockSpec((2, 1, levels // parts, 128), lambda q, p: (0, q, p, 0)),
+            pl.BlockSpec((2, 1, levels, 128), lambda q: (0, q, 0, 0)),
             full(cols),
             full(sides),
             full(depth),
@@ -507,8 +520,10 @@
         out_specs=block,
         out_shape=jax.ShapeDtypeStruct(base.shape, f32),
         scratch_shapes=[
-            pltpu.VMEM((8, o_rows + 16, 128), f32),
-            pltpu.VMEM((levels, o_rows, 128), f32),
+            [V((group, o_rows + 16, 128), f32)] * 2,
+            [V((group * o_rows, 256), bf16)] * 2,
+            [V((group * o_rows, 128), f32)] * 2,
+            V((levels, o_rows, 128), f32),
         ],
         compiler_params=pltpu.CompilerParams(vmem_limit_bytes=VMEM_BYTES),
         name="finish",

time: 63.4 us -> 44.9 us (0.71)
  Pallas kernels: 63.2 us -> 44.3 us
    pallas_call x1, Pallas kernels: 46.2 us -> 35.2 us  [couple(): pl.pallas_call(functools.partial(couple_kernel, n_lat, n_lon), in_specs=[...]
    pallas_call x1, Pallas kernels: 17.1 us -> 9.11 us  [finish(): pl.pallas_call(finish_kernel, grid=(q_count,), in_specs=[block, full(forc...]
where the time goes in v4:
time: 44.9 us; the launch traced here: 44.3 us
  Pallas kernels  44.3 us (99%)
    pallas_call x1, Pallas kernels, couple(): pl.pallas_call(functools.partial(couple_kernel, n_lat, n_lon), in_specs=[...  35.2 us
    pallas_call x1, Pallas kernels, finish(): pl.pallas_call(finish_kernel, grid=(q_count,), in_specs=[block, full(forc...  9.11 us

profile of v4, /device:TPU:0, one launch (start us, length us, event | category | flops | bytes accessed | tf_op | source)
XLA Modules:
  0.0 44.3 jit_solution(17652303823151455855)
XLA Ops:
  0.0 35.2 %couple.1 = (f32[4,80,32,128]{3,2,1,0:T(8,128)}, f32[128,128]{1,0:T(8,128)}, f32[128,128]{1,0:T(8,128)}, f32[2,4,80,128]{3,2,1,0:T(8,128)}, f32[2,128,128]{2,1,0:T(8,128)}, /*index=5*/s32[4,32,128]{2,1,0:T(8,128)}) custom-call(s32[256]{0:T(256)} %src_ref.1, f32[4,8]{1,0:T(4,128)} %coupling_ref.1, s32[1,256]{1,0:T(1,128)} %bitcast.4, s32[1,256]{1,0:T(1,128)} %bitcast.5, ...), custom_call_target="tpu_custom_call" | custom-call | tf_op jit(solution)/shard_map/couple/pallas_call | solution.py:390
  35.2 9.1 %finish.1 = f32[4,80,32,128]{3,2,1,0:T(8,128)} custom-call(f32[4,80,32,128]{3,2,1,0:T(8,128)} %get-tuple-element.11.base_ref, f32[128,128]{1,0:T(8,128)} %get-tuple-element.12.force_ref, f32[128,128]{1,0:T(8,128)} %get-tuple-element.13.gain_ref, f32[2,4,80,128]{3,2,1,0:T(8,128)} %get-tuple-element.14.rows_ref, f32[2,128,128]{2,1,0:T(8,128)} %get-tuple-element.15.cols_ref, ...), custom_call_target="tpu_custom_call" | custom-call | tf_op jit(solution)/shard_map/finish/pallas_call | solution.py:508

commit v5 on v4

--- a/solution.py
+++ b/solution.py
@@ -37,12 +37,12 @@
     n_lat, n_lon,
     src_ref, coupling_ref, dest_ref, block_ref, atm_ref, mask_ref, depth_ref,
     weights_hbm, inverses_hbm, ocean_hbm,
-    base_hbm, force_ref, gain_ref, rows_ref, cols_ref, sides_ref,
+    base_hbm, keep_hbm, force_ref, gains_ref, rows_ref, cols_ref,
     weights, inverses, ocean, skewed, table, contrib,
     send, meta, recv, recv_meta, partial, partial_in,
-    packed, col_out, gain_out, force_out, strip_out, row_out,
-    row_in, col_in, gain_in, gain_strip_in, depth_in, force_in, strip_in,
-    load_sems, ship_sems, row_sems, halo_send, halo_recv, force_send, force_recv,
+    packed, col_out, gain_ref, gain_out, force_out, strip_out, row_out,
+    row_in, col_in, gain_in, gain_strip_in, depth_in, force_in, strip_in, sides_ref, keep,
+    load_sems, ship_sems, row_sems, depth_sems, halo_send, halo_recv, force_send, force_recv,
 ):
     chips = n_lat * n_lon // 2
     devices = 2 * chips
@@ -103,8 +103,9 @@
 
     for dz in range(n_lat):
         plane(dz, greet)
-    for side in (WEST, EAST):
-        pl.semaphore_signal(barrier, inc=1, device_id=beside[side], device_id_type=MESH)
+    slant = [(beside[side][0], partner[1]) for side in (NORTH, SOUTH)]
+    for other in (beside[WEST], beside[EAST], *slant):
+        pl.semaphore_signal(barrier, inc=1, device_id=other, device_id_type=MESH)
 
     a_rows = mask_ref.shape[0]
     mask = mask_ref[...].astype(f32)
@@ -178,11 +179,21 @@
                 :, h * 128 : (h + 1) * 128
             ].reshape(chunk // 8, 8, 128)
 
+    depth_copies = [
+        pltpu.make_async_remote_copy(
+            depth_ref, depth_in.at[(SOUTH, NORTH, EAST, WEST)[side]],
+            depth_sems.at[side], depth_sems.at[4 + side],
+            device_id=beside[side], device_id_type=MESH,
+        )
+        for side in range(4)
+    ]
     mine = pl.ds(2 * my_chip, 2)
     for n, dz in enumerate(ORDER):
         place(lax.rem(lat + dz, n_lat))
         if n == 0:
-            pl.semaphore_wait(barrier, chips + 1)
+            pl.semaphore_wait(barrier, chips + 3)
+            for copy in depth_copies:
+                copy.start()
 
         def ship(z, o):
             to = z * (n_lon // 2) + o // 2
@@ -276,13 +287,44 @@
         copy.start()
         copies.append(copy)
 
-    for side in range(4):
-        hand(side, depth_ref, lambda o: depth_in.at[o])
     for side in (NORTH, SOUTH):
         hand(side, gain_out.at[side], lambda o: gain_strip_in.at[o])
     for side in (WEST, EAST):
         hand(side, col_out.at[side - 2], lambda o: col_in.at[o - 2])
         hand(side, gain_ref, lambda o: gain_in.at[o - 2])
+
+    for copy in depth_copies:
+        copy.wait()
+    depth = depth_ref[...]
+    in_band = (lat > 0).astype(i32), (lat < n_lat - 1).astype(i32)
+    north_depth = depth_in[NORTH] * in_band[0]
+    south_depth = depth_in[SOUTH] * in_band[1]
+    row_id, cell_id = iota(depth.shape, 0), iota(depth.shape, 1)
+    roll = pltpu.roll
+    sides_ref[NORTH] = jnp.where(row_id == 0, roll(north_depth, 1, 0), roll(depth, 1, 0))
+    sides_ref[SOUTH] = jnp.where(
+        row_id == o_rows - 1, roll(south_depth, o_rows - 1, 0), roll(depth, o_rows - 1, 0)
+    )
+    sides_ref[WEST] = jnp.where(cell_id == 0, roll(depth_in[WEST], 1, 1), roll(depth, 1, 1))
+    sides_ref[EAST] = jnp.where(cell_id == 127, roll(depth_in[EAST], 127, 1), roll(depth, 127, 1))
+
+    def weigh(l, carry):
+        count = jnp.zeros(depth.shape, f32)
+        for s in range(4):
+            count = count + jnp.where(l < sides_ref[s], diffusion_rate, 0.0)
+        keep[l] = 1.0 - count
+        return carry
+
+    lax.fori_loop(0, levels, weigh, 0, unroll=4)
+    keep_copy = pltpu.make_async_copy(keep, keep_hbm, load_sems.at[w_chunks + 2 + q_count])
+    keep_copy.start()
+    for q in range(q_count):
+        gain = packed[2, low_levels, :]
+        gain = gain if q == 0 else roll(gain, 128 - q * o_rows, 1)
+        high, low = (part.astype(f32) for part in halves(gain))
+        third = lane_id // o_rows
+        gain = jnp.where(third == 0, high, jnp.where(third == 1, roll(low, 32, 1), roll(high, 64, 1)))
+        gains_ref[q] = jnp.where(third == 3, 0.0, gain)
 
     partial[...] = jnp.zeros_like(partial)
     per_plane = chips // n_lat
@@ -303,26 +345,33 @@
             out = dot(hot, both) if out is None else out + dot(hot, both)
         partial[...] += (out[:, :128] + out[:, 128:]).reshape(2, 128, 128)
 
-    swap = pltpu.make_async_remote_copy(
-        partial.at[1 - core], partial_in, force_send.at[4], force_recv.at[4],
-        device_id=partner, device_id_type=MESH,
-    )
-    swap.start()
-    swap.wait()
-    force = partial[core] + partial_in[...]
-    force_ref[...] = force
-    for s, r in ((0, 0), (1, o_rows - 1)):
-        force_out[s, pl.ds(0, q_count), :] = force_ref[pl.ds(r, q_count, stride=o_rows), :]
-    force_t = jnp.transpose(force)
-    strip_out[0, pl.ds(0, 1), :] = force_t[:1]
-    strip_out[1, pl.ds(0, 1), :] = force_t[127:]
+    own, other = partial[core], partial[1 - core]
+    for e, mine_or in enumerate((core, 1 - core)):
+        for side, r in ((0, 0), (1, o_rows - 1)):
+            force_out[e, side, pl.ds(0, q_count), :] = partial[
+                mine_or, pl.ds(r, q_count, stride=o_rows), :
+            ]
+    turned, turned_other = jnp.transpose(own), jnp.transpose(other)
+    on_left = core == 0
+    strip_out[0, pl.ds(0, 1), :] = turned[:1]
+    strip_out[1, pl.ds(0, 1), :] = turned[127:]
+    strip_out[2, pl.ds(0, 1), :] = jnp.where(on_left, turned_other[127:], turned_other[:1])
+    inner = jnp.where(on_left, turned_other[:1], turned_other[127:])
+    hops = [
+        (partial.at[1 - core], partial_in, partner),
+        (force_out.at[0, 0], force_in.at[0, 1], beside[NORTH]),
+        (force_out.at[0, 1], force_in.at[0, 0], beside[SOUTH]),
+        (force_out.at[1, 0], force_in.at[1, 1], slant[0]),
+        (force_out.at[1, 1], force_in.at[1, 0], slant[1]),
+        (strip_out.at[0], strip_in.at[1], beside[WEST]),
+        (strip_out.at[1], strip_in.at[0], beside[EAST]),
+        (strip_out.at[2], strip_in.at[2], (lat, lax.rem(lon + n_lon + 2 - 4 * core, n_lon))),
+    ]
     forces = []
-    for side in range(4):
-        opposite = (SOUTH, NORTH, EAST, WEST)[side]
-        out, into = (force_out, force_in) if side < 2 else (strip_out, strip_in)
+    for n, (source, target, device) in enumerate(hops):
         copy = pltpu.make_async_remote_copy(
-            out.at[side % 2], into.at[opposite % 2], force_send.at[side], force_recv.at[side],
-            device_id=beside[side], device_id_type=MESH,
+            source, target, force_send.at[n], force_recv.at[n],
+            device_id=device, device_id_type=MESH,
         )
         copy.start()
         forces.append(copy)
@@ -332,18 +381,6 @@
     for q in range(q_count):
         for side in (NORTH, SOUTH):
             row_copy(side, q).wait()
-    depth = depth_ref[...]
-    in_band = (lat > 0).astype(i32), (lat < n_lat - 1).astype(i32)
-    north_depth = depth_in[NORTH] * in_band[0]
-    south_depth = depth_in[SOUTH] * in_band[1]
-    row_id, cell_id = iota(depth.shape, 0), iota(depth.shape, 1)
-    roll = pltpu.roll
-    sides_ref[NORTH] = jnp.where(row_id == 0, roll(north_depth, 1, 0), roll(depth, 1, 0))
-    sides_ref[SOUTH] = jnp.where(
-        row_id == o_rows - 1, roll(south_depth, o_rows - 1, 0), roll(depth, o_rows - 1, 0)
-    )
-    sides_ref[WEST] = jnp.where(cell_id == 0, roll(depth_in[WEST], 1, 1), roll(depth, 1, 1))
-    sides_ref[EAST] = jnp.where(cell_id == 127, roll(depth_in[EAST], 127, 1), roll(depth, 127, 1))
     limits = [
         jnp.concatenate([jnp.broadcast_to(edge, (o_rows, 128))] * q_count, axis=0)
         for edge in (depth_in[WEST][:, 127:], depth_in[EAST][:, :1])
@@ -355,16 +392,21 @@
     )
     for copy in forces:
         copy.wait()
+    force_ref[...] = own + partial_in[...]
     edges = north_depth[o_rows - 1 :], south_depth[:1]
     for s in range(2):
         for q in range(q_count):
             gain = jnp.broadcast_to(strips[:levels, s * 8 + q : s * 8 + q + 1], (levels, 128))
-            value = row_in[s, q] + gain * force_in[s, pl.ds(q, 1), :]
+            force = force_in[0, s, pl.ds(q, 1), :] + force_in[1, s, pl.ds(q, 1), :]
+            value = row_in[s, q] + gain * force
             rows_ref[s, q] = jnp.where(level < edges[s], value, 0.0)
     level_lane = iota((128, 128), 1)
     edge = []
     for s in range(2):
-        strip = jnp.transpose(jnp.broadcast_to(strip_in[s, pl.ds(0, 1), :], (128, 128)))
+        outer = strip_in[2, pl.ds(0, 1), :]
+        rest_of = jnp.where(on_left, *((outer, inner) if s == 0 else (inner, outer)))
+        strip = strip_in[s, pl.ds(0, 1), :] + rest_of
+        strip = jnp.transpose(jnp.broadcast_to(strip, (128, 128)))
         value = col_in[s] + gain_in[s] * strip
         edge.append(jnp.where(level_lane < limits[s], value, 0.0))
     cols_ref[0] = jnp.where(level_lane < 64, edge[0], roll(edge[1], 64, 1))
@@ -376,6 +418,7 @@
     pltpu.make_async_copy(meta.at[rest], meta.at[rest], meta_send_sem).wait()
     for q in range(q_count):
         copy_out(q).wait()
+    keep_copy.wait()
 
 
 def couple(src, coupling, dest, block, atm, mask, depth, weights, inverses, ocean, n_lat, n_lon):
@@ -390,14 +433,14 @@
     return pl.pallas_call(
         functools.partial(couple_kernel, n_lat, n_lon),
         in_specs=[smem, smem] + [vmem] * 5 + [hbm] * 3,
-        out_specs=[hbm] + [vmem] * 5,
+        out_specs=[hbm] * 2 + [vmem] * 4,
         out_shape=[
             shape((q_count, levels, o_rows, 128), f32),
+            shape((levels, o_rows, 128), f32),
             shape((128, 128), f32),
-            shape((128, 128), f32),
+            shape((q_count, levels, 128), f32),
             shape((2, q_count, levels, 128), f32),
             shape((2, 128, 128), f32),
-            shape((4, o_rows, 128), i32),
         ],
         scratch_shapes=[
             V(weights.shape, bf16),
@@ -414,24 +457,28 @@
             V((128, 128), f32),
             V((3, 128, 128), f32),
             V((2, 128, 128), f32),
+            V((128, 128), f32),
             V((2, 8, 128), f32),
-            V((2, 8, 128), f32),
-            V((2, 8, 128), f32),
+            V((2, 2, 8, 128), f32),
+            V((3, 8, 128), f32),
             V((2, q_count, levels, 128), f32),
             V((2, q_count, levels, 128), f32),
             V((2, 128, 128), f32),
             V((2, 128, 128), f32),
             V((2, 8, 128), f32),
             V((4, o_rows, 128), i32),
-            V((2, 8, 128), f32),
-            V((2, 8, 128), f32),
-            DMA((14,)),
+            V((2, 2, 8, 128), f32),
+            V((3, 8, 128), f32),
+            V((4, o_rows, 128), i32),
+            V((levels, o_rows, 128), f32),
+            DMA((15,)),
             DMA((10,)),
             DMA((4, q_count)),
+            DMA((8,)),
             DMA((12,)),
             DMA((12,)),
-            DMA((5,)),
-            DMA((5,)),
+            DMA((8,)),
+            DMA((8,)),
         ],
         compiler_params=pltpu.CompilerParams(
             collective_id=0, has_side_effects=True, vmem_limit_bytes=VMEM_BYTES
@@ -441,65 +488,65 @@
 
 
 def finish_kernel(
-    base_ref, force_ref, gain_ref, rows_ref, cols_ref, sides_ref, depth_ref, out_ref,
-    slabs, splits, sums, keep,
+    base_ref, keep_ref, force_ref, gains_ref, rows_ref, cols_ref, depth_ref, out_ref,
+    slabs, splits, sums, spots, forced,
 ):
     q = pl.program_id(0)
     levels, o_rows = base_ref.shape[1:3]
-    shape = (o_rows, 128)
-    cell = iota(shape, 1)
+    cell = iota((o_rows, 128), 1)
     here = pl.ds(q * o_rows, o_rows)
     group = slabs[0].shape[0]
     groups = levels // group
-    first, last = cell == 0, cell == 127
-    rim = first | last
-    far = jnp.where(last, 64, 0)
+    rim = (cell == 0) | (cell == 127)
+    far = jnp.where(cell == 127, 64, 0)
+    own_row = cell % o_rows == iota((o_rows, 128), 0)
     apart = iota((256, 128), 0) % 128 - iota((256, 128), 1)
     beside = one_hot((apart == 1) | (apart == -1))
-
-    @pl.when(q == 0)
-    def _():
-        def weigh(l, carry):
-            count = jnp.zeros(shape, f32)
-            for s in range(4):
-                count = count + jnp.where(l < sides_ref[s], diffusion_rate, 0.0)
-            keep[l] = 1.0 - count
-            return carry
-
-        lax.fori_loop(0, levels, weigh, 0, unroll=4)
+    high, low = halves(force_ref[here, :])
+    forces = jnp.concatenate([high, high, low, jnp.zeros_like(low)], axis=0)
+
+    def tile(j):
+        return pl.ds(j * o_rows, o_rows)
+
+    def spot(n, j):
+        gain = gains_ref[0, pl.ds(n * group + j, 1), :]
+        spots[n % 2][tile(j), :] = jnp.where(own_row, gain, 0.0).astype(bf16)
 
     def force(n, j):
         slab, split, l = slabs[n % 2], splits[n % 2], n * group + j
-        gain = jnp.take_along_axis(gain_ref[here, :], jnp.full(shape, l, i32), axis=1)
-        mixed = base_ref[0, l] + gain * force_ref[here, :]
+        mixed = base_ref[0, l] + forced[n % 2][tile(j), :]
         mixed = jnp.where(l < depth_ref[...], mixed, 0.0)
         slab[j, pl.ds(8, o_rows), :] = mixed
         slab[j, pl.ds(7, 1), :] = rows_ref[0, 0, pl.ds(l, 1), :]
         slab[j, pl.ds(8 + o_rows, 1), :] = rows_ref[1, 0, pl.ds(l, 1), :]
         high, low = halves(mixed)
-        split[pl.ds(j * o_rows, o_rows), pl.ds(0, 128)] = high
-        split[pl.ds(j * o_rows, o_rows), pl.ds(128, 128)] = low
+        split[tile(j), pl.ds(0, 128)] = high
+        split[tile(j), pl.ds(128, 128)] = low
 
     def spread(n, j):
-        slab, total, l = slabs[n % 2], sums[n % 2], n * group + j
+        slab, l = slabs[n % 2], n * group + j
         edge = jnp.take_along_axis(cols_ref[l // 64, here, :], far + l % 64, axis=1)
         near = slab[j, pl.ds(7, o_rows), :] + slab[j, pl.ds(9, o_rows), :]
-        near = near + total[pl.ds(j * o_rows, o_rows), :]
+        near = near + sums[n % 2][tile(j), :]
         near = near + jnp.where(rim, edge, 0.0)
-        value = keep[l] * slab[j, pl.ds(8, o_rows), :] + diffusion_rate * near
+        value = keep_ref[l] * slab[j, pl.ds(8, o_rows), :] + diffusion_rate * near
         out_ref[0, l] = jnp.where(l < depth_ref[...], value, base_ref[0, l])
 
-    for j in range(group):
-        force(0, j)
-    for n in range(groups):
-        sums[n % 2][...] = dot(splits[n % 2][...], beside)
+    for n in range(-2, groups):
+        if n >= 0:
+            sums[n % 2][...] = dot(splits[n % 2][...], beside)
+        if 0 <= n + 1 < groups:
+            forced[(n + 1) % 2][...] = dot(spots[(n + 1) % 2][...], forces)
         for j in range(group):
-            if n + 1 < groups:
+            if n + 2 < groups:
+                spot(n + 2, j)
+            if n >= 0:
+                spread(n, j)
+            if 0 <= n + 1 < groups:
                 force(n + 1, j)
-            spread(n, j)
-
-
-def finish(base, force, gain, rows, cols, sides, depth):
+
+
+def finish(base, keep, force, gains, rows, cols, depth):
     q_count, levels, o_rows, _ = base.shape
     group = 16
     full = lambda a: pl.BlockSpec(a.shape, lambda q: (0,) * a.ndim)
@@ -510,11 +557,11 @@
         grid=(q_count,),
         in_specs=[
             block,
+            full(keep),
             full(force),
-            full(gain),
+            pl.BlockSpec((1, levels, 128), lambda q: (q, 0, 0)),
             pl.BlockSpec((2, 1, levels, 128), lambda q: (0, q, 0, 0)),
             full(cols),
-            full(sides),
             full(depth),
         ],
         out_specs=block,
@@ -523,11 +570,12 @@
             [V((group, o_rows + 16, 128), f32)] * 2,
             [V((group * o_rows, 256), bf16)] * 2,
             [V((group * o_rows, 128), f32)] * 2,
-            V((levels, o_rows, 128), f32),
+            [V((group * o_rows, 128), bf16)] * 2,
+            [V((group * o_rows, 128), f32)] * 2,
         ],
         compiler_params=pltpu.CompilerParams(vmem_limit_bytes=VMEM_BYTES),
         name="finish",
-    )(base, force, gain, rows, cols, sides, depth)
+    )(base, keep, force, gains, rows, cols, depth)
 
 
 def on_device(
@@ -545,13 +593,13 @@
     n_lat, n_lon = lax.axis_size("lat"), lax.axis_size("lon")
     pairs = src_block.shape[0]
     q_count, levels, o_rows, cells = ocean_state.shape
-    base, force, gain, rows, cols, sides = couple(
+    base, keep, force, gains, rows, cols = couple(
         src_block, coupling, dest_dev.reshape(1, pairs), dest_block.reshape(1, pairs),
         atm_flux, sea_mask, depth_levels, intersection_weights,
         inverses.reshape(q_count, o_rows, levels, levels),
         ocean_state, n_lat, n_lon,
     )
-    return finish(base, force, gain, rows, cols, sides, depth_levels)
+    return finish(base, keep, force, gains, rows, cols, depth_levels)
 
 
 def solution(mesh):

time: 44.9 us -> 44.2 us (0.984)
  the two profiles are of different devices: /device:TPU:0 before, /device:TPU:1 now
where the time goes in v5:
time: 44.2 us; the launch traced here: 43.9 us
  Pallas kernels  43.9 us (99%)
    pallas_call x1, Pallas kernels, couple(): pl.pallas_call(functools.partial(couple_kernel, n_lat, n_lon), in_specs=[...  35.6 us
    pallas_call x1, Pallas kernels, finish(): pl.pallas_call(finish_kernel, grid=(q_count,), in_specs=[block, full(keep...  8.34 us

profile of v5, /device:TPU:1, one launch (start us, length us, event | category | flops | bytes accessed | tf_op | source)
XLA Modules:
  0.0 43.9 jit_solution(15592312096470758038)
XLA Ops:
  0.0 35.6 %couple.1 = (f32[4,80,32,128]{3,2,1,0:T(8,128)}, f32[80,32,128]{2,1,0:T(8,128)}, f32[128,128]{1,0:T(8,128)}, f32[4,80,128]{2,1,0:T(8,128)}, f32[2,4,80,128]{3,2,1,0:T(8,128)}, /*index=5*/f32[2,128,128]{2,1,0:T(8,128)}) custom-call(s32[256]{0:T(256)} %src_ref.1, f32[4,8]{1,0:T(4,128)} %coupling_ref.1, s32[1,256]{1,0:T(1,128)} %bitcast.4, s32[1,256]{1,0:T(1,128)} %bitcast.5, ...), custom_call_target="tpu_custom_call" | custom-call | tf_op jit(solution)/shard_map/couple/pallas_call | solution.py:433
  35.6 8.3 %finish.1 = f32[4,80,32,128]{3,2,1,0:T(8,128)} custom-call(f32[4,80,32,128]{3,2,1,0:T(8,128)} %get-tuple-element.11.base_ref, f32[80,32,128]{2,1,0:T(8,128)} %get-tuple-element.12.keep_ref, f32[128,128]{1,0:T(8,128)} %get-tuple-element.13.force_ref, f32[4,80,128]{2,1,0:T(8,128)} %get-tuple-element.14.gains_ref, ...), custom_call_target="tpu_custom_call" | custom-call | tf_op jit(solution)/shard_map/finish/pallas_call | solution.py:555

commit v6 on v5

--- a/solution.py
+++ b/solution.py
@@ -11,7 +11,7 @@
 CAP = 4
 MESH = pl.DeviceIdType.MESH
 NORTH, SOUTH, WEST, EAST = range(4)
-ORDER = (2, 1, 3, 0)
+ORDER = (1, 3, 2, 0)
 f32, bf16, i32 = jnp.float32, jnp.bfloat16, jnp.int32
 VMEM_BYTES = 62 << 20
 
@@ -73,22 +73,15 @@
 
     x_here, y_here = lon // 8, lon // 2 % 4
 
-    def plane(dz, each, first=0):
+    xs = [lax.rem(x_here + dx, 4) * 8 + core for dx in range(4)]
+    ys = [lax.rem(y_here + dy, 4) * 2 for dy in range(4)]
+
+    def plane(dz, each):
         z = lax.rem(lat + dz, n_lat)
-        xs = [lax.rem(x_here + dx, 4) * 8 + core for dx in range(4)]
-
-        def line(dy, carry):
-            y = lax.rem(y_here + dy, 4) * 2
+        for dy in range(4):
             for dx in range(4):
-                each(z, xs[dx] + y)
-            return carry
-
-        if dz == 0:
-            for dx in range(1, 4):
-                each(z, xs[dx] + y_here * 2)
-            lax.fori_loop(1, 4, line, 0)
-        else:
-            lax.fori_loop(0, 4, line, 0)
+                if dx or dy or dz:
+                    each(z, xs[dx] + ys[dy])
 
     beside = {
         NORTH: ((lat + n_lat - 1) % n_lat, lon),
@@ -101,7 +94,7 @@
     def greet(z, o):
         pl.semaphore_signal(barrier, inc=1, device_id=(z, o), device_id_type=MESH)
 
-    for dz in range(n_lat):
+    for dz in (2, 1, 3, 0):
         plane(dz, greet)
     slant = [(beside[side][0], partner[1]) for side in (NORTH, SOUTH)]
     for other in (beside[WEST], beside[EAST], *slant):

time: 44.2 us -> 41.8 us (0.946)
  the two profiles are of different devices: /device:TPU:1 before, /device:TPU:0 now
where the time goes in v6:
time: 41.8 us; the launch traced here: 41.3 us
  Pallas kernels  41.3 us (99%)
    pallas_call x1, Pallas kernels, couple(): pl.pallas_call(functools.partial(couple_kernel, n_lat, n_lon), in_specs=[...  32.9 us
    pallas_call x1, Pallas kernels, finish(): pl.pallas_call(finish_kernel, grid=(q_count,), in_specs=[block, full(keep...  8.34 us

profile of v6, /device:TPU:0, one launch (start us, length us, event | category | flops | bytes accessed | tf_op | source)
XLA Modules:
  0.0 41.3 jit_solution(14330283382085213807)
XLA Ops:
  0.0 32.9 %couple.1 = (f32[4,80,32,128]{3,2,1,0:T(8,128)}, f32[80,32,128]{2,1,0:T(8,128)}, f32[128,128]{1,0:T(8,128)}, f32[4,80,128]{2,1,0:T(8,128)}, f32[2,4,80,128]{3,2,1,0:T(8,128)}, /*index=5*/f32[2,128,128]{2,1,0:T(8,128)}) custom-call(s32[256]{0:T(256)} %src_ref.1, f32[4,8]{1,0:T(4,128)} %coupling_ref.1, s32[1,256]{1,0:T(1,128)} %bitcast.4, s32[1,256]{1,0:T(1,128)} %bitcast.5, ...), custom_call_target="tpu_custom_call" | custom-call | tf_op jit(solution)/shard_map/couple/pallas_call | solution.py:426
  32.9 8.3 %finish.1 = f32[4,80,32,128]{3,2,1,0:T(8,128)} custom-call(f32[4,80,32,128]{3,2,1,0:T(8,128)} %get-tuple-element.11.base_ref, f32[80,32,128]{2,1,0:T(8,128)} %get-tuple-element.12.keep_ref, f32[128,128]{1,0:T(8,128)} %get-tuple-element.13.force_ref, f32[4,80,128]{2,1,0:T(8,128)} %get-tuple-element.14.gains_ref, ...), custom_call_target="tpu_custom_call" | custom-call | tf_op jit(solution)/shard_map/finish/pallas_call | solution.py:548

commit v7 on v6

--- a/solution.py
+++ b/solution.py
@@ -66,8 +66,6 @@
         weight_copy(c).start()
     inverse_copy = pltpu.make_async_copy(inverses_hbm, inverses, load_sems.at[w_chunks])
     ocean_copy = pltpu.make_async_copy(ocean_hbm, ocean, load_sems.at[w_chunks + 1])
-    inverse_copy.start()
-    ocean_copy.start()
 
     barrier = pltpu.get_barrier_semaphore()
 
@@ -152,7 +150,11 @@
 
         return lax.fori_loop(0, w_size // 4, four, carry, unroll=4)
 
-    lax.fori_loop(0, w_chunks, chunk_of_pairs, 0)
+    early = w_chunks - 2
+    lax.fori_loop(0, early, chunk_of_pairs, 0)
+    inverse_copy.start()
+    ocean_copy.start()
+    lax.fori_loop(early, w_chunks, chunk_of_pairs, 0)
 
     high, low = halves(
         jnp.concatenate(
@@ -541,7 +543,7 @@
 
 def finish(base, keep, force, gains, rows, cols, depth):
     q_count, levels, o_rows, _ = base.shape
-    group = 16
+    group = 20
     full = lambda a: pl.BlockSpec(a.shape, lambda q: (0,) * a.ndim)
     block = pl.BlockSpec((1, levels, o_rows, 128), lambda q: (q, 0, 0, 0))
     V = pltpu.VMEM

time: 41.8 us -> 41.7 us (level)
  no operation moved by 1% of the time
where the time goes in v7:
time: 41.7 us; the launch traced here: 41.2 us
  Pallas kernels  41.2 us (99%)
    pallas_call x1, Pallas kernels, couple(): pl.pallas_call(functools.partial(couple_kernel, n_lat, n_lon), in_specs=[...  32.9 us
    pallas_call x1, Pallas kernels, finish(): pl.pallas_call(finish_kernel, grid=(q_count,), in_specs=[block, full(keep...  8.26 us

profile of v7, /device:TPU:0, one launch (start us, length us, event | category | flops | bytes accessed | tf_op | source)
XLA Modules:
  0.0 41.2 jit_solution(15606868713815334105)
XLA Ops:
  0.0 32.9 %couple.1 = (f32[4,80,32,128]{3,2,1,0:T(8,128)}, f32[80,32,128]{2,1,0:T(8,128)}, f32[128,128]{1,0:T(8,128)}, f32[4,80,128]{2,1,0:T(8,128)}, f32[2,4,80,128]{3,2,1,0:T(8,128)}, /*index=5*/f32[2,128,128]{2,1,0:T(8,128)}) custom-call(s32[256]{0:T(256)} %src_ref.1, f32[4,8]{1,0:T(4,128)} %coupling_ref.1, s32[1,256]{1,0:T(1,128)} %bitcast.4, s32[1,256]{1,0:T(1,128)} %bitcast.5, ...), custom_call_target="tpu_custom_call" | custom-call | tf_op jit(solution)/shard_map/couple/pallas_call | solution.py:428
  32.9 8.3 %finish.1 = f32[4,80,32,128]{3,2,1,0:T(8,128)} custom-call(f32[4,80,32,128]{3,2,1,0:T(8,128)} %get-tuple-element.11.base_ref, f32[80,32,128]{2,1,0:T(8,128)} %get-tuple-element.12.keep_ref, f32[128,128]{1,0:T(8,128)} %get-tuple-element.13.force_ref, f32[4,80,128]{2,1,0:T(8,128)} %get-tuple-element.14.gains_ref, ...), custom_call_target="tpu_custom_call" | custom-call | tf_op jit(solution)/shard_map/finish/pallas_call | solution.py:550

commit v8 on v7

--- a/solution.py
+++ b/solution.py
@@ -55,18 +55,6 @@
     skew = skewed.shape[0] // levels
     o_rows = depth_ref.shape[0]
 
-    w_chunks = 8
-    w_size = pairs // w_chunks
-
-    def weight_copy(c):
-        part = pl.ds(c * w_size, w_size)
-        return pltpu.make_async_copy(weights_hbm.at[part], weights.at[part], load_sems.at[c])
-
-    for c in range(w_chunks):
-        weight_copy(c).start()
-    inverse_copy = pltpu.make_async_copy(inverses_hbm, inverses, load_sems.at[w_chunks])
-    ocean_copy = pltpu.make_async_copy(ocean_hbm, ocean, load_sems.at[w_chunks + 1])
-
     barrier = pltpu.get_barrier_semaphore()
 
     x_here, y_here = lon // 8, lon // 2 % 4
@@ -97,6 +85,18 @@
     slant = [(beside[side][0], partner[1]) for side in (NORTH, SOUTH)]
     for other in (beside[WEST], beside[EAST], *slant):
         pl.semaphore_signal(barrier, inc=1, device_id=other, device_id_type=MESH)
+
+    w_chunks = 8
+    w_size = pairs // w_chunks
+
+    def weight_copy(c):
+        part = pl.ds(c * w_size, w_size)
+        return pltpu.make_async_copy(weights_hbm.at[part], weights.at[part], load_sems.at[c])
+
+    for c in range(w_chunks):
+        weight_copy(c).start()
+    inverse_copy = pltpu.make_async_copy(inverses_hbm, inverses, load_sems.at[w_chunks])
+    ocean_copy = pltpu.make_async_copy(ocean_hbm, ocean, load_sems.at[w_chunks + 1])
 
     a_rows = mask_ref.shape[0]
     mask = mask_ref[...].astype(f32)

time: 41.7 us -> 42.2 us (1.012)
  Pallas kernels: 41.2 us -> 42 us
    pallas_call x1, Pallas kernels: 32.9 us -> 33.7 us  [couple(): pl.pallas_call(functools.partial(couple_kernel, n_lat, n_lon), in_specs=[...]
where the time goes in v8:
time: 42.2 us; the launch traced here: 42 us
  Pallas kernels  42 us (100%)
    pallas_call x1, Pallas kernels, couple(): pl.pallas_call(functools.partial(couple_kernel, n_lat, n_lon), in_specs=[...  33.7 us
    pallas_call x1, Pallas kernels, finish(): pl.pallas_call(finish_kernel, grid=(q_count,), in_specs=[block, full(keep...  8.25 us

profile of v8, /device:TPU:0, one launch (start us, length us, event | category | flops | bytes accessed | tf_op | source)
XLA Modules:
  0.0 42.0 jit_solution(16091823503311960583)
XLA Ops:
  0.0 33.7 %couple.1 = (f32[4,80,32,128]{3,2,1,0:T(8,128)}, f32[80,32,128]{2,1,0:T(8,128)}, f32[128,128]{1,0:T(8,128)}, f32[4,80,128]{2,1,0:T(8,128)}, f32[2,4,80,128]{3,2,1,0:T(8,128)}, /*index=5*/f32[2,128,128]{2,1,0:T(8,128)}) custom-call(s32[256]{0:T(256)} %src_ref.1, f32[4,8]{1,0:T(4,128)} %coupling_ref.1, s32[1,256]{1,0:T(1,128)} %bitcast.4, s32[1,256]{1,0:T(1,128)} %bitcast.5, ...), custom_call_target="tpu_custom_call" | custom-call | tf_op jit(solution)/shard_map/couple/pallas_call | solution.py:428
  33.7 8.3 %finish.1 = f32[4,80,32,128]{3,2,1,0:T(8,128)} custom-call(f32[4,80,32,128]{3,2,1,0:T(8,128)} %get-tuple-element.11.base_ref, f32[80,32,128]{2,1,0:T(8,128)} %get-tuple-element.12.keep_ref, f32[128,128]{1,0:T(8,128)} %get-tuple-element.13.force_ref, f32[4,80,128]{2,1,0:T(8,128)} %get-tuple-element.14.gains_ref, ...), custom_call_target="tpu_custom_call" | custom-call | tf_op jit(solution)/shard_map/finish/pallas_call | solution.py:550

commit v9 on v7

--- a/solution.py
+++ b/solution.py
@@ -543,7 +543,7 @@
 
 def finish(base, keep, force, gains, rows, cols, depth):
     q_count, levels, o_rows, _ = base.shape
-    group = 20
+    group = 16
     full = lambda a: pl.BlockSpec(a.shape, lambda q: (0,) * a.ndim)
     block = pl.BlockSpec((1, levels, o_rows, 128), lambda q: (q, 0, 0, 0))
     V = pltpu.VMEM

time: 41.7 us -> 41.8 us (level)
  no operation moved by 1% of the time
where the time goes in v9:
time: 41.8 us; the launch traced here: 41.3 us
  Pallas kernels  41.3 us (99%)
    pallas_call x1, Pallas kernels, couple(): pl.pallas_call(functools.partial(couple_kernel, n_lat, n_lon), in_specs=[...  32.9 us
    pallas_call x1, Pallas kernels, finish(): pl.pallas_call(finish_kernel, grid=(q_count,), in_specs=[block, full(keep...  8.34 us

profile of v9, /device:TPU:0, one launch (start us, length us, event | category | flops | bytes accessed | tf_op | source)
XLA Modules:
  0.0 41.3 jit_solution(3028462793634719989)
XLA Ops:
  0.0 32.9 %couple.1 = (f32[4,80,32,128]{3,2,1,0:T(8,128)}, f32[80,32,128]{2,1,0:T(8,128)}, f32[128,128]{1,0:T(8,128)}, f32[4,80,128]{2,1,0:T(8,128)}, f32[2,4,80,128]{3,2,1,0:T(8,128)}, /*index=5*/f32[2,128,128]{2,1,0:T(8,128)}) custom-call(s32[256]{0:T(256)} %src_ref.1, f32[4,8]{1,0:T(4,128)} %coupling_ref.1, s32[1,256]{1,0:T(1,128)} %bitcast.4, s32[1,256]{1,0:T(1,128)} %bitcast.5, ...), custom_call_target="tpu_custom_call" | custom-call | tf_op jit(solution)/shard_map/couple/pallas_call | solution.py:428
  32.9 8.3 %finish.1 = f32[4,80,32,128]{3,2,1,0:T(8,128)} custom-call(f32[4,80,32,128]{3,2,1,0:T(8,128)} %get-tuple-element.11.base_ref, f32[80,32,128]{2,1,0:T(8,128)} %get-tuple-element.12.keep_ref, f32[128,128]{1,0:T(8,128)} %get-tuple-element.13.force_ref, f32[4,80,128]{2,1,0:T(8,128)} %get-tuple-element.14.gains_ref, ...), custom_call_target="tpu_custom_call" | custom-call | tf_op jit(solution)/shard_map/finish/pallas_call | solution.py:550
